TPU v7x, 1024 devices: a whole 4x8x16 slice. The times are simulated.
1024 devices in a mesh: pole: 8 (over x, core), grid: 128 (over z, y).
Axes of the slice: x: 4, y: 8, z: 16, core: 2. Of those that a mesh axis runs over, the one named last changes fastest.
Arguments:
- trailing: bfloat16 [8, 2, 4096, 4096], P('pole', None, 'grid'), may hold values from -4.5 to 4.5, as said below
- panel: bfloat16 [8, 2, 4096, 256], P('pole', None, 'grid'), may hold values from -0.0625 to 0.0625
- diag_inverse: bfloat16 [8, 2, 256, 256], P('pole', None, 'grid'), may hold values from -6 to 6
- pole_weights: float32 [8, 2], P('pole'), may hold values from -2 to 2
- owner_map: int32 [4096, 1], P('grid'), may hold values from 0 to 7; in each aligned block of 32 rows (0 to 31, 32 to 63, ...) at most 8 rows name the same one
- ham_slab: bfloat16 [256, 4096], replicated, may hold values from -0.375 to 0.375
Outputs:
- density_diag: float32 [256, 256], P('grid')
- patch_energy: bfloat16 [8192, 4096], P(('pole', 'grid'))
Inputs may be any that keep to these rules, and one draw needn't show every extreme that they name: trailing is symmetric in its last two dimensions: trailing[p, c, i, j] = trailing[p, c, j, i]. `owner_map`: in each aligned block of 32 rows (the rows of one index of grid) at most 8 rows name the same owner, and some block reaches 8.
All inputs are finite; a program needn't handle non-finite values.
Results may differ from a plain program's by a relative error of at most 0.011.
Values may be sent and summed in bfloat16 or wider, within the bound.
No kernel may reach another device: no remote copies, remote signals or barrier semaphores. Data moves between devices by JAX's collectives and lax.ppermute only.
A program may use at most 32 MiB of HBM per device.

v0:
```python
import jax
import jax.numpy as jnp
from jax import lax
from jax.sharding import PartitionSpec as P


def complex_product(left_real, left_imag, right_real, right_imag, form):

    def product(first, second):
        return jnp.einsum(form, first, second, preferred_element_type=jnp.float32)

    real = product(left_real, right_real) - product(left_imag, right_imag)
    imag = product(left_real, right_imag) + product(left_imag, right_real)
    return (real, imag)


def per_device(trailing, panel, diag_inverse, pole_weights, owner_map, ham_slab):
    rows_here = trailing.shape[2]
    width = panel.shape[3]
    piece = lax.all_gather(panel, "grid", axis=2, tiled=True)
    real, imag = complex_product(
        trailing[:, 0], trailing[:, 1], piece[:, 0], piece[:, 1], "prn,pnw->prw"
    )
    cross_real = (-real).astype(jnp.bfloat16)
    cross_imag = (-imag).astype(jnp.bfloat16)
    weight_real = pole_weights[:, 0][:, None, None]
    weight_imag = pole_weights[:, 1][:, None, None]
    density_rows = jnp.sum(
        weight_real * cross_imag.astype(jnp.float32) + weight_imag * cross_real.astype(jnp.float32),
        axis=0,
    )
    quad_real, quad_imag = complex_product(
        panel[:, 0], panel[:, 1], cross_real, cross_imag, "prw,prv->pwv"
    )
    quad_part = -jnp.sum(weight_real * quad_imag + weight_imag * quad_real, axis=0)
    diag_term = jnp.sum(
        weight_real * diag_inverse[:, 1].astype(jnp.float32)
        + weight_imag * diag_inverse[:, 0].astype(jnp.float32),
        axis=0,
    )
    block_rows = diag_inverse.shape[2]
    offset = lax.axis_index("grid") * block_rows
    padded = lax.dynamic_update_slice_in_dim(
        jnp.zeros((width, width), jnp.float32), diag_term, offset, 0
    )
    total = lax.psum(quad_part + padded, ("pole", "grid"))
    density_diag = lax.dynamic_slice_in_dim(total, offset, block_rows, 0)
    owners = owner_map[:, 0]
    capacity = 2 * rows_here // lax.axis_size("pole")
    same = owners[:, None] == owners[None, :]
    earlier = lax.broadcasted_iota(jnp.int32, (rows_here, rows_here), 1) < lax.broadcasted_iota(
        jnp.int32, (rows_here, rows_here), 0
    )
    rank = jnp.sum((same & earlier).astype(jnp.int32), axis=1)
    slot = owners * capacity + rank
    all_slots = lax.axis_size("pole") * capacity
    placement = (
        slot[:, None] == lax.broadcasted_iota(jnp.int32, (rows_here, all_slots), 1)
    ).astype(jnp.float32)
    total_rows = lax.psum(density_rows, "pole")
    chosen = lax.dynamic_slice_in_dim(placement, lax.axis_index("pole") * capacity, capacity, 1)
    owned_rows = jnp.einsum("rs,rw->sw", chosen, total_rows, precision=lax.Precision.HIGHEST)
    patch = owned_rows.astype(jnp.bfloat16)
    patch_energy = jnp.dot(patch, ham_slab, preferred_element_type=jnp.float32).astype(jnp.bfloat16)
    return (density_diag, patch_energy)


def solution(mesh):
    placed = (
        P("pole", None, "grid", None),
        P("pole", None, "grid", None),
        P("pole", None, "grid", None),
        P("pole", None),
        P("grid", None),
        P(),
    )
    return jax.shard_map(
        per_device,
        mesh=mesh,
        in_specs=placed,
        out_specs=(P("grid", None), P(("pole", "grid"), None)),
        check_vma=False,
    )
```

profile of v0, /device:TPU:1, one launch (start us, length us, event | category | flops | bytes accessed | tf_op | source)
XLA Modules:
  0.0 669.8 jit_solution(2472276346642811302)
XLA Ops:
  7.2 0.0 copy-start
  7.2 0.0 copy-start.5
  7.2 0.0 all-gather.2.cloned.1.call-start
  7.2 0.7 all-gather.2.cloned.1.call-update
  7.9 0.0 all-reduce.2.cloned.1.call-start
  8.0 1.3 fusion.37
  9.3 0.9 convert_reduce_fusion
  10.2 0.7 fusion.36
  10.9 0.0 copy-start.2
  10.9 152.2 %all-gather.2.cloned.1.call-done = bf16[1,2,4096,256]{3,2,1,0:T(8,128)(2,1)} async-done(((bf16[1,2,32,256]{3,2,1,0:T(8,128)(2,1)}), bf16[1,2,4096,256]{3,2,1,0:T(8,128)(2,1)}) %all-gather.2.cloned.1.call-update) | async-done | bytes 4194320 | tf_op jit(solution)/shard_map/all_gather | solution.py:20
  163.1 0.0 copy-start.4
  163.1 2.3 fusion.1
  165.3 0.0 copy-done.5
  165.4 2.1 fusion.13
  167.4 0.0 copy-done.2
  167.4 0.2 fusion.26
  167.7 0.0 copy-done.4
  167.7 0.5 fusion
  168.1 0.0 copy-start.3
  168.2 1.8 multiply_add_fusion
  169.9 0.2 fusion.24
  170.2 0.9 fusion.7
  171.1 0.9 fusion.6
  172.0 0.0 copy-done.3
  172.0 1.3 fusion.35
  173.3 0.0 copy-start.1
  173.3 0.7 copy-done.1
  174.0 0.0 all-reduce.2.cloned.1.call-update
  174.0 28.9 %psum.15 = f32[32,256]{1,0:T(8,128)S(1)} all-reduce(f32[32,256]{1,0:T(8,128)S(1)} %get-tuple-element.4), channel_id=1, replica_groups=mesh['pole'=8,'grid'=128] {'pole'}, use_global_device_ids=true, to_apply=%region_2.0 | all-reduce | flops 8192 | bytes 65536 | tf_op jit(solution)/shard_map/psum | solution.py:60
  202.9 0.3 convolution_convert_fusion.1
  203.1 0.0 copy-done
  203.1 1.0 convolution_convert_fusion
  204.2 457.5 %all-reduce.2.cloned.1.call-done = f32[256,256]{1,0:T(8,128)} async-done(((f32[256,256]{1,0:T(8,128)}), f32[256,256]{1,0:T(8,128)}) %all-reduce.2.cloned.1.call-update) | async-done | bytes 262160 | tf_op jit(solution)/shard_map/psum | solution.py:46
  661.7 1.3 constant_dynamic-slice_fusion
  (1 shorter events, 0.0 us)
Async XLA Ops:
  7.2 196.0 %copy-start = (bf16[256,4096]{1,0:T(8,128)(2,1)S(1)}, bf16[256,4096]{1,0:T(8,128)(2,1)}, u32[]{:S(2)}) copy-start(bf16[256,4096]{1,0:T(8,128)(2,1)} %param.11) | copy-start | bytes 6291460
  7.2 158.2 %copy-start.5 = (bf16[1,2,32,4096]{3,2,1,0:T(8,128)(2,1)S(1)}, bf16[1,2,32,4096]{3,2,1,0:T(8,128)(2,1)}, u32[]{:S(2)}) copy-start(bf16[1,2,32,4096]{3,2,1,0:T(8,128)(2,1)} %param.6) | copy-start | bytes 1572868
  7.2 155.9 %all-gather.2.cloned.1.call-start = ((), (), s32[]{:S(2)}) async-start(), calls=%async_computation | async-start | bytes 4227072 | tf_op jit(solution)/shard_map/all_gather | solution.py:20
  7.9 653.8 %all-reduce.2.cloned.1.call-start = ((), (), s32[]{:S(2)}) async-start(), calls=%async_computation.1 | async-start | bytes 524288 | tf_op jit(solution)/shard_map/psum | solution.py:46
  10.9 156.6 %copy-start.2 = (bf16[1,2,32,256]{3,2,1,0:T(8,128)(2,1)S(1)}, bf16[1,2,32,256]{3,2,1,0:T(8,128)(2,1)}, u32[]{:S(2)}) copy-start(bf16[1,2,32,256]{3,2,1,0:T(8,128)(2,1)} %param.7) | copy-start | bytes 98308
  163.1 4.6 copy-start.4
  168.1 3.8 copy-start.3
  173.3 0.7 copy-start.1
Sparse Core Ops, SparseCore 0:
  12.1 150.8 all-gather.1
  174.1 487.5 all-reduce.1
where the time goes:
time: 672 us; the launch traced here: 670 us
  waiting for transfers between devices  610 us (91%)
  blocking collectives  28.9 us (4%)
  between operations  14.2 us (2%)
  matrix products  10.1 us (2%)
    psum x1, waiting for transfers between devices, per_device(): total = lax.psum(quad_part + padded, ('pole', 'grid'))  458 us
    all_gather x1, waiting for transfers between devices, per_device(): piece = lax.all_gather(panel, 'grid', axis=2, tiled=True)  152 us
    psum x1, blocking collectives, per_device(): total_rows = lax.psum(density_rows, 'pole')  28.9 us
  transfers between devices with their start and end apart: 2, of which 2 were waited for; matrix products, arithmetic and copies ran while one was open for 1% of the time, Pallas kernels for 0%

commit v1 on v0

v1 whole, which is shorter than its diff:
```python
import jax
import jax.numpy as jnp
from jax import lax
from jax.experimental import pallas as pl
from jax.experimental.pallas import tpu as pltpu
from jax.sharding import Mesh, PartitionSpec as P

NX, NC, NZ, NY = 4, 2, 16, 8
NP = NX * NC
RD = 32
W = 256
ZR = NY * RD
YC = NZ * RD
CAP = 8
F32 = jnp.float32
BF16 = jnp.bfloat16
VM = pl.BlockSpec(memory_space=pltpu.VMEM)
SM = pl.BlockSpec(memory_space=pltpu.SMEM)


def kernel_call(body, outs, specs, name, flops=0, moved=0):
    shapes = tuple(jax.ShapeDtypeStruct(s, d) for s, d in outs)
    return pl.pallas_call(
        body,
        out_shape=shapes,
        in_specs=specs,
        out_specs=tuple(VM for _ in outs),
        name=name,
        cost_estimate=pl.CostEstimate(flops=flops, bytes_accessed=moved, transcendentals=0),
    )


def pack_kernel(g_ref, l_ref, out_ref, own_ref):
    quarter = lax.broadcasted_iota(jnp.int32, (RD, 128), 1) // 32
    for part in range(2):
        for half in range(2):
            for tile in range(4):
                loaded = [
                    g_ref[0, part, :, (4 * tile + j) * W + half * 128 : (4 * tile + j) * W + half * 128 + 128].astype(F32)
                    for j in range(4)
                ]
                for q in range(4):
                    joined = None
                    for j in range(4):
                        shift = (32 * (j - q)) % 128
                        moved = pltpu.roll(loaded[j], shift, 1) if shift else loaded[j]
                        joined = moved if joined is None else jnp.where(quarter == j, moved, joined)
                    out_ref[4 * half + q, RD * part : RD * part + RD, 128 * tile : 128 * tile + 128] = joined.astype(BF16)
    for part in range(2):
        rows = l_ref[0, part]
        own_ref[:, W * part : W * part + W] = rows
        for y in range(NY):
            out_ref[y, 2 * RD : 3 * RD, W * part : W * part + W] = rows


def cross_kernel(w_ref, b_ref, l_ref, out_ref):
    wr = w_ref[0, 0]
    wi = w_ref[0, 1]
    columns = l_ref[...].reshape(YC, 2 * W)
    first = jnp.dot(b_ref[:, 0:RD, :].reshape(ZR, YC), columns, preferred_element_type=F32)
    second = jnp.dot(b_ref[:, RD : 2 * RD, :].reshape(ZR, YC), columns, preferred_element_type=F32)
    real = first[:, :W] - second[:, W:]
    imag = first[:, W:] + second[:, :W]
    even = wr * imag + wi * real
    odd = wr * real - wi * imag
    rows = b_ref[:, 2 * RD : 3 * RD, :].reshape(ZR, 2 * W)
    over_rows = (((0,), (0,)), ((), ()))
    quad = lax.dot_general(rows[:, :W], even.astype(BF16), over_rows, preferred_element_type=F32)
    quad = quad + lax.dot_general(rows[:, W:], odd.astype(BF16), over_rows, preferred_element_type=F32)
    to = lax.broadcasted_iota(jnp.int32, (W, W), 0)
    source = (to % 32) // 2 * 16 + to // 32 * 2 + to % 2
    order = (lax.broadcasted_iota(jnp.int32, (W, W), 1) == source).astype(F32).astype(BF16)
    quad = jnp.dot(order, quad.astype(BF16), preferred_element_type=F32).astype(BF16)
    density = (-even).astype(BF16)
    for y in range(NY):
        out_ref[y, :, 0:W] = density[RD * y : RD * y + RD]
        out_ref[y, :, W : 2 * W] = quad[RD * y : RD * y + RD]


def slot_kernel(o_ref, p_ref, slots_ref, quad_ref):
    total = jnp.sum(p_ref[...].astype(F32), axis=0)
    owner = jnp.broadcast_to(o_ref[...], (RD, RD))
    row = lax.broadcasted_iota(jnp.int32, (RD, RD), 0)
    column = lax.broadcasted_iota(jnp.int32, (RD, RD), 1)
    owner_down = jnp.sum(jnp.where(row == column, owner, 0), axis=1, keepdims=True)
    earlier = (owner_down == owner) & (row < column)
    rank = jnp.sum(earlier.astype(jnp.int32), axis=0, keepdims=True)
    slot = o_ref[...] * CAP + rank
    place = (lax.broadcasted_iota(jnp.int32, (NP * CAP, RD), 0) == slot).astype(F32)
    slots = jnp.dot(place, total[:, :W], precision=lax.Precision.HIGHEST, preferred_element_type=F32)
    for k in range(NP):
        slots_ref[k] = slots[CAP * k : CAP * k + CAP]
    for z in range(NZ):
        quad_ref[z] = total[2 * z : 2 * z + 2, W : 2 * W]


def join_kernel(w_ref, q_ref, d_ref, s_ref, out_ref):
    quad = jnp.sum(q_ref[...], axis=0)
    quad = quad + w_ref[0, 0] * d_ref[0, 1].astype(F32) + w_ref[0, 1] * d_ref[0, 0].astype(F32)
    zero = jnp.zeros((CAP - 2, W), F32)
    for k in range(NP):
        out_ref[k, 0:CAP] = s_ref[k]
        out_ref[k, CAP : CAP + 2] = quad
        out_ref[k, CAP + 2 :] = zero


def energy_kernel(p_ref, h_ref, diag_ref, energy_ref):
    total = jnp.sum(p_ref[...], axis=0)
    half = total[0:CAP].astype(BF16)
    energy_ref[...] = jnp.dot(half, h_ref[...], preferred_element_type=F32).astype(BF16)
    diag_ref[...] = total[CAP : CAP + 2]


def per_device(trailing, panel, diag_inverse, pole_weights, owner_map, ham_slab):
    packed, own = kernel_call(
        pack_kernel, [((NY, 3 * RD, YC), BF16), ((RD, 2 * W), BF16)], [VM, VM], "pack", moved=1 << 20
    )(trailing, panel)
    columns = lax.all_gather(own, "z")
    block = lax.all_to_all(packed, "y", 0, 0)
    (partial,) = kernel_call(
        cross_kernel, [((NY, RD, 2 * W), BF16)], [SM, VM, VM], "cross", flops=1 << 29, moved=1 << 20
    )(pole_weights, block, columns)
    partial = lax.all_to_all(partial, "y", 0, 0)
    slots, quad = kernel_call(
        slot_kernel, [((NP, CAP, W), F32), ((NZ, 2, W), F32)], [VM, VM], "slot", moved=1 << 18
    )(owner_map.reshape(1, RD), partial)
    quad = lax.all_to_all(quad, "z", 0, 0)
    (joined,) = kernel_call(
        join_kernel, [((NP, 2 * CAP, W), F32)], [SM, VM, VM, VM], "join", moved=1 << 18
    )(pole_weights, quad, diag_inverse, slots)
    joined = lax.all_to_all(joined, ("x", "c"), 0, 0)
    density_diag, patch_energy = kernel_call(
        energy_kernel, [((2, W), F32), ((CAP, NZ * NY * RD), BF16)], [VM, VM], "energy", flops=1 << 24, moved=1 << 21
    )(joined, ham_slab)
    return (density_diag, patch_energy)


def solution(mesh):
    fine = Mesh(mesh.devices.reshape(NX, NC, NZ, NY), ("x", "c", "z", "y"))
    pole, grid = ("x", "c"), ("z", "y")
    by_row = P(pole, None, grid, None)
    return jax.shard_map(
        per_device,
        mesh=fine,
        in_specs=(by_row, by_row, by_row, P(pole, None), P(grid, None), P()),
        out_specs=(P(grid, None), P(("x", "c", "z", "y"), None)),
        check_vma=False,
    )
```

time: 672 us -> 114 us (0.17)
  waiting for transfers between devices: 610 us -> 0.01 us
  blocking collectives: 28.9 us -> 92.8 us
  between operations: 14.2 us -> 0.64 us
  Pallas kernels: 0 us -> 11.5 us
  matrix products: 10.1 us -> 0 us
  starting transfers between devices: 0.08 us -> 7.64 us
    psum x1 -> x0, waiting for transfers between devices: 458 us -> none  [per_device(): total = lax.psum(quad_part + padded, ('pole', 'grid'))]
    all_gather x1 -> x0, waiting for transfers between devices: 152 us -> none  [per_device(): piece = lax.all_gather(panel, 'grid', axis=2, tiled=True)]
    all_to_all x0 -> x3, blocking collectives: none -> 51.9 us  [the longest x1 19.9 us: per_device(): joined = lax.all_to_all(joined, ('x', 'c'), 0, 0)]
    all_gather x0 -> x1, blocking collectives: none -> 40.9 us  [per_device(): columns = lax.all_gather(own, 'z')]
    psum x1 -> x0, blocking collectives: 28.9 us -> none  [per_device(): total_rows = lax.psum(density_rows, 'pole')]
    pallas_call x0 -> x5, Pallas kernels: none -> 11.5 us  [the longest x1 2.93 us: per_device(): kernel_call(cross_kernel, [((NY, RD, 2 * W), BF16)], [SM, VM, VM], 'cross...]
    dot_general x10 -> x0, matrix products: 10.1 us -> none  [the longest x8 8.78 us: product(): return jnp.einsum(form, first, second, preferred_element_type=jnp.float32)]
    all_to_all x0 -> x1, starting transfers between devices: none -> 7.64 us  [per_device(): block = lax.all_to_all(packed, 'y', 0, 0)]
  transfers between devices with their start and end apart: 2 -> 1, of which waited for: 2 -> 0; matrix products, arithmetic and copies ran while one was open for 1% -> 0% of each run, Pallas kernels for 0% -> 0%
where the time goes in v1:
time: 114 us; the launch traced here: 113 us
  blocking collectives  92.8 us (81%)
  Pallas kernels  11.5 us (10%)
  starting transfers between devices  7.64 us (7%)
    all_gather x1, blocking collectives, per_device(): columns = lax.all_gather(own, 'z')  40.9 us
    all_to_all x1, blocking collectives, per_device(): joined = lax.all_to_all(joined, ('x', 'c'), 0, 0)  19.9 us
    all_to_all x1, blocking collectives, per_device(): partial = lax.all_to_all(partial, 'y', 0, 0)  16.3 us
    all_to_all x1, blocking collectives, per_device(): quad = lax.all_to_all(quad, 'z', 0, 0)  15.7 us
    all_to_all x1, starting transfers between devices, per_device(): block = lax.all_to_all(packed, 'y', 0, 0)  7.64 us
    pallas_call x1, Pallas kernels, per_device(): kernel_call(cross_kernel, [((NY, RD, 2 * W), BF16)], [SM, VM, VM], 'cross...  2.93 us
    pallas_call x1, Pallas kernels, per_device(): kernel_call(energy_kernel, [((2, W), F32), ((CAP, NZ * NY * RD), BF16)],...  2.69 us
    pallas_call x1, Pallas kernels, per_device(): kernel_call(pack_kernel, [((NY, 3 * RD, YC), BF16), ((RD, 2 * W), BF16)],...  2.42 us
  transfers between devices with their start and end apart: 1, of which 0 were waited for; matrix products, arithmetic and copies ran while one was open for 0% of the time, Pallas kernels for 0%

profile of v1, /device:TPU:1, one launch (start us, length us, event | category | flops | bytes accessed | tf_op | source)
XLA Modules:
  0.0 113.5 jit_solution(2173961788767099986)
XLA Ops:
  0.6 2.4 %pack.1 = (bf16[8,96,512]{2,1,0:T(8,128)(2,1)}, bf16[32,512]{1,0:T(8,128)(2,1)}) custom-call(bf16[1,2,32,4096]{3,2,1,0:T(8,128)(2,1)} %g_ref.1, bf16[1,2,32,256]{3,2,1,0:T(8,128)(2,1)} %l_ref.1), custom_call_target="tpu_custom_call" | custom-call | bytes 1048576 | tf_op jit(solution)/shard_map/pack/pallas_call | solution.py:115
  3.1 7.6 %all-to-all-start = ((bf16[8,96,512]{2,1,0:T(8,128)(2,1)}), bf16[8,96,512]{2,1,0:T(8,128)(2,1)S(1)}, u32[]{:S(2)}, u32[]{:S(2)}) async-start(bf16[8,96,512]{2,1,0:T(8,128)(2,1)} %get-tuple-element.6), calls=%async_computation | async-start | bytes 1572864 | tf_op jit(solution)/shard_map/all_to_all | solution.py:119
  10.7 40.9 %all-gather = bf16[512,512]{1,0:T(8,128)(2,1)} all-gather(bf16[32,512]{1,0:T(8,128)(2,1)} %get-tuple-element.7), channel_id=2, replica_groups=mesh['x'=4,'c'=2,'z'=16,'y'=8] {'z'}, dimensions={0}, use_global_device_ids=true | all-gather | bytes 557056 | tf_op jit(solution)/shard_map/all_gather | solution.py:118
  51.6 0.0 all-to-all-done.b_ref
  51.6 0.0 copy-start
  51.6 0.9 copy-done
  52.5 2.9 %cross.1 = bf16[8,32,512]{2,1,0:T(8,128)(2,1)} custom-call(f32[1,2]{1,0:T(1,128)} %w_ref.3, bf16[8,96,512]{2,1,0:T(8,128)(2,1)} %copy-done, bf16[16,32,512]{2,1,0:T(8,128)(2,1)} %bitcast.2), custom_call_target="tpu_custom_call" | custom-call | flops 536870912 | bytes 1048576 | tf_op jit(solution)/shard_map/cross/pallas_call | solution.py:120
  55.4 16.3 %all_to_all.20.p_ref = bf16[8,32,512]{2,1,0:T(8,128)(2,1)} all-to-all(bf16[8,32,512]{2,1,0:T(8,128)(2,1)} %cross.1), channel_id=1, replica_groups=mesh['x'=4,'c'=2,'z'=16,'y'=8] {'y'}, dimensions={0} | all-to-all | bytes 524288 | tf_op jit(solution)/shard_map/all_to_all | solution.py:123
  71.7 1.9 %slot.1 = (f32[8,8,256]{2,1,0:T(8,128)}, f32[16,2,256]{2,1,0:T(2,128)}) custom-call(s32[1,32]{1,0:T(1,128)} %bitcast.3, bf16[8,32,512]{2,1,0:T(8,128)(2,1)} %all_to_all.20.p_ref), custom_call_target="tpu_custom_call" | custom-call | bytes 262144 | tf_op jit(solution)/shard_map/slot/pallas_call | solution.py:124
  73.6 15.7 %all_to_all.21.q_ref = f32[16,2,256]{2,1,0:T(2,128)} all-to-all(f32[16,2,256]{2,1,0:T(2,128)} %get-tuple-element.8), channel_id=1, replica_groups=mesh['x'=4,'c'=2,'z'=16,'y'=8] {'z'}, dimensions={0} | all-to-all | bytes 65536 | tf_op jit(solution)/shard_map/all_to_all | solution.py:127
  89.3 1.6 %join.1 = f32[8,16,256]{2,1,0:T(8,128)} custom-call(f32[1,2]{1,0:T(1,128)} %w_ref.3, f32[16,2,256]{2,1,0:T(2,128)} %all_to_all.21.q_ref, bf16[1,2,2,256]{3,2,1,0:T(2,128)(2,1)} %d_ref.1, f32[8,8,256]{2,1,0:T(8,128)} %get-tuple-element.9.s_ref), custom_call_target="tpu_custom_call" | custom-call | bytes 262144 | tf_op jit(solution)/shard_map/join/pallas_call | solution.py:128
  90.9 19.9 %all_to_all.22.p_ref = f32[8,16,256]{2,1,0:T(8,128)} all-to-all(f32[8,16,256]{2,1,0:T(8,128)} %join.1), channel_id=1, replica_groups=mesh['x'=4,'c'=2,'z'=16,'y'=8] {'x','c'}, dimensions={0} | all-to-all | bytes 262144 | tf_op jit(solution)/shard_map/all_to_all | solution.py:131
  110.8 2.7 %energy.1 = (f32[2,256]{1,0:T(2,128)}, bf16[8,4096]{1,0:T(8,128)(2,1)}) custom-call(f32[8,16,256]{2,1,0:T(8,128)} %all_to_all.22.p_ref, bf16[256,4096]{1,0:T(8,128)(2,1)} %h_ref.1), custom_call_target="tpu_custom_call" | custom-call | flops 16777216 | bytes 2097152 | tf_op jit(solution)/shard_map/energy/pallas_call | solution.py:132
Async XLA Ops:
  3.1 48.6 %all-to-all-start = ((bf16[8,96,512]{2,1,0:T(8,128)(2,1)}), bf16[8,96,512]{2,1,0:T(8,128)(2,1)S(1)}, u32[]{:S(2)}, u32[]{:S(2)}) async-start(bf16[8,96,512]{2,1,0:T(8,128)(2,1)} %get-tuple-element.6), calls=%async_computation | async-start | bytes 1572864 | tf_op jit(solution)/shard_map/all_to_all | solution.py:119
  51.6 0.9 copy-start

commit v2 on v1

v2 whole, which is shorter than its diff:
```python
import jax
import jax.numpy as jnp
from jax import lax
from jax.experimental import pallas as pl
from jax.experimental.pallas import tpu as pltpu
from jax.sharding import Mesh, PartitionSpec as P

NX, NC, NZ, NY = 4, 2, 16, 8
NP = NX * NC
RD = 32
W = 256
ZR = NY * RD
YC = NZ * RD
CAP = 8
TAIL = 16
F32 = jnp.float32
BF16 = jnp.bfloat16
VM = pl.BlockSpec(memory_space=pltpu.VMEM)
SM = pl.BlockSpec(memory_space=pltpu.SMEM)


def kernel_call(body, outs, specs, flops=0, moved=0):
    shapes = tuple(jax.ShapeDtypeStruct(s, d) for s, d in outs)
    return pl.pallas_call(
        body,
        out_shape=shapes,
        in_specs=specs,
        out_specs=tuple(VM for _ in outs),
        cost_estimate=pl.CostEstimate(flops=flops, bytes_accessed=moved, transcendentals=0),
    )


def pack_kernel(o_ref, g_ref, l_ref, out_ref, own_ref):
    owner = jnp.broadcast_to(o_ref[...], (RD, RD))
    row = lax.broadcasted_iota(jnp.int32, (RD, RD), 0)
    column = lax.broadcasted_iota(jnp.int32, (RD, RD), 1)
    owner_down = jnp.sum(jnp.where(row == column, owner, 0), axis=1, keepdims=True)
    earlier = (owner_down == owner) & (row < column)
    rank = jnp.sum(earlier.astype(jnp.int32), axis=0, keepdims=True)
    slot = (o_ref[...] * CAP + rank).astype(F32)
    slot = jnp.broadcast_to(slot, (TAIL, RD)).astype(BF16)
    for y in range(NY):
        out_ref[y, 3 * RD :, :] = jnp.zeros((TAIL, YC), BF16)
        out_ref[y, 3 * RD :, 0:RD] = slot
    quarter = lax.broadcasted_iota(jnp.int32, (RD, 128), 1) // 32
    for part in range(2):
        for half in range(2):
            for tile in range(4):
                loaded = [
                    g_ref[0, part, :, (4 * tile + j) * W + half * 128 : (4 * tile + j) * W + half * 128 + 128].astype(F32)
                    for j in range(4)
                ]
                for q in range(4):
                    joined = None
                    for j in range(4):
                        shift = (32 * (j - q)) % 128
                        moved = pltpu.roll(loaded[j], shift, 1) if shift else loaded[j]
                        joined = moved if joined is None else jnp.where(quarter == j, moved, joined)
                    out_ref[4 * half + q, RD * part : RD * part + RD, 128 * tile : 128 * tile + 128] = joined.astype(BF16)
    for part in range(2):
        rows = l_ref[0, part]
        own_ref[:, W * part : W * part + W] = rows
        for y in range(NY):
            out_ref[y, 2 * RD : 3 * RD, W * part : W * part + W] = rows


def cross_kernel(w_ref, b_ref, l_ref, density_ref, quad_ref):
    wr = w_ref[0, 0]
    wi = w_ref[0, 1]
    columns = l_ref[...].reshape(YC, 2 * W)
    first = jnp.dot(b_ref[:, 0:RD, :].reshape(ZR, YC), columns, preferred_element_type=F32)
    second = jnp.dot(b_ref[:, RD : 2 * RD, :].reshape(ZR, YC), columns, preferred_element_type=F32)
    real = first[:, :W] - second[:, W:]
    imag = first[:, W:] + second[:, :W]
    even = wr * imag + wi * real
    odd = wr * real - wi * imag
    rows = b_ref[:, 2 * RD : 3 * RD, :].reshape(ZR, 2 * W)
    over_rows = (((0,), (0,)), ((), ()))
    quad = lax.dot_general(rows[:, :W], even.astype(BF16), over_rows, preferred_element_type=F32)
    quad = quad + lax.dot_general(rows[:, W:], odd.astype(BF16), over_rows, preferred_element_type=F32)
    quad_ref[...] = quad.astype(BF16).reshape(NZ, W // NZ, W)
    density_ref[...] = (-even).astype(BF16)


def place_kernel(s_ref, density_ref, out_ref):
    index = lax.broadcasted_iota(jnp.int32, (NP * CAP, RD), 0)
    for y in range(NY):
        slot = s_ref[y, 0:1, 0:RD].astype(F32).astype(jnp.int32)
        place = (index == slot).astype(F32).astype(BF16)
        rows = density_ref[RD * y : RD * y + RD, :]
        placed = jnp.dot(place, rows, preferred_element_type=F32).astype(BF16)
        for k in range(NP):
            out_ref[NY * k + y] = placed[CAP * k : CAP * k + CAP]


def join_kernel(w_ref, q_ref, d_ref, p_ref, out_ref):
    quad = jnp.sum(q_ref[...].astype(F32), axis=0)
    diag = w_ref[0, 0] * d_ref[0, 1].astype(F32) + w_ref[0, 1] * d_ref[0, 0].astype(F32)
    here = lax.axis_index("y")
    zero = jnp.zeros((CAP - 4, 128), F32)
    for y in range(NY):
        rows = quad[2 * y : 2 * y + 2] + jnp.where(here == y, diag, 0.0)
        tail = jnp.concatenate([rows[:, :128], rows[:, 128:], zero], axis=0).astype(BF16)
        for k in range(NP):
            out_ref[NY * k + y, :, 0:W] = p_ref[NY * k + y]
            out_ref[NY * k + y, :, W:] = tail


def energy_kernel(p_ref, h_ref, diag_ref, energy_ref):
    total = jnp.sum(p_ref[...].astype(F32), axis=0)
    half = total[:, :W].astype(BF16)
    energy_ref[...] = jnp.dot(half, h_ref[...], preferred_element_type=F32).astype(BF16)
    diag_ref[:, 0:128] = total[0:2, W:]
    diag_ref[:, 128:] = total[2:4, W:]


def per_device(trailing, panel, diag_inverse, pole_weights, owner_map, ham_slab):
    packed, own = kernel_call(
        pack_kernel, [((NY, 3 * RD + TAIL, YC), BF16), ((RD, 2 * W), BF16)], [VM] * 3, moved=1 << 20
    )(owner_map.reshape(1, RD), trailing, panel)
    block = lax.all_to_all(packed, "y", 0, 0)
    columns = lax.all_gather(own, "z")
    density, quad = kernel_call(
        cross_kernel, [((ZR, W), BF16), ((NZ, W // NZ, W), BF16)], [SM, VM, VM], flops=1 << 29, moved=1 << 20
    )(pole_weights, block, columns)
    quad = lax.all_to_all(quad, "z", 0, 0)
    (placed,) = kernel_call(
        place_kernel, [((NP * NY, CAP, W), BF16)], [VM, VM], flops=1 << 23, moved=1 << 18
    )(block[:, 3 * RD :, :128], density)
    (joined,) = kernel_call(
        join_kernel, [((NP * NY, CAP, W + 128), BF16)], [SM, VM, VM, VM], moved=1 << 18
    )(pole_weights, quad, diag_inverse, placed)
    joined = lax.all_to_all(joined, ("x", "c", "y"), 0, 0)
    density_diag, patch_energy = kernel_call(
        energy_kernel, [((2, W), F32), ((CAP, NZ * NY * RD), BF16)], [VM, VM], flops=1 << 24, moved=1 << 21
    )(joined, ham_slab)
    return (density_diag, patch_energy)


def solution(mesh):
    fine = Mesh(mesh.devices.reshape(NX, NC, NZ, NY), ("x", "c", "z", "y"))
    pole, grid = ("x", "c"), ("z", "y")
    by_row = P(pole, None, grid, None)
    return jax.shard_map(
        per_device,
        mesh=fine,
        in_specs=(by_row, by_row, by_row, P(pole, None), P(grid, None), P()),
        out_specs=(P(grid, None), P(("x", "c", "z", "y"), None)),
        check_vma=False,
    )
```

time: 114 us -> 111 us (0.974)
  blocking collectives: 92.8 us -> 75.4 us
  waiting for transfers between devices: 0.01 us -> 8.83 us
  starting transfers between devices: 7.64 us -> 11.3 us
  local copies, waits for them, and re-layouts: 0.89 us -> 2.98 us
    all_to_all x3 -> x1, blocking collectives: 51.9 us -> 33.9 us  [per_device(): joined = lax.all_to_all(joined, ('x', 'c', 'y'), 0, 0)]
    all_to_all x0 -> x1, waiting for transfers between devices: none -> 8.83 us  [per_device(): quad = lax.all_to_all(quad, 'z', 0, 0)]
    all_to_all x0 -> x1, starting transfers between devices: none -> 3.67 us  [per_device(): quad = lax.all_to_all(quad, 'z', 0, 0)]
    slice x0 -> x1, local copies, waits for them, and re-layouts: none -> 1.38 us  [per_device(): block[:, 3 * RD:, :128]]
  transfers between devices with their start and end apart: 1 -> 2, of which waited for: 0 -> 1; matrix products, arithmetic and copies ran while one was open for 0% -> 1% of each run, Pallas kernels for 0% -> 2%
where the time goes in v2:
time: 111 us
  blocking collectives  75.4 us (68%)
  Pallas kernels  11.7 us (11%)
  starting transfers between devices  11.3 us (10%)
  waiting for transfers between devices  8.83 us (8%)
  local copies, waits for them, and re-layouts  2.98 us (3%)
    all_gather x1, blocking collectives, per_device(): columns = lax.all_gather(own, 'z')  41.5 us
    all_to_all x1, blocking collectives, per_device(): joined = lax.all_to_all(joined, ('x', 'c', 'y'), 0, 0)  33.9 us
    all_to_all x1, waiting for transfers between devices, per_device(): quad = lax.all_to_all(quad, 'z', 0, 0)  8.83 us
    all_to_all x1, starting transfers between devices, per_device(): block = lax.all_to_all(packed, 'y', 0, 0)  7.64 us
    all_to_all x1, starting transfers between devices, per_device(): quad = lax.all_to_all(quad, 'z', 0, 0)  3.67 us
    pallas_call x1, Pallas kernels, per_device(): kernel_call(energy_kernel, [((2, W), F32), ((CAP, NZ * NY * RD), BF16)],...  2.81 us
    pallas_call x1, Pallas kernels, per_device(): kernel_call(cross_kernel, [((ZR, W), BF16), ((NZ, W // NZ, W), BF16)], [S...  2.74 us
    pallas_call x1, Pallas kernels, per_device(): kernel_call(pack_kernel, [((NY, 3 * RD + TAIL, YC), BF16), ((RD, 2 * W),...  2.5 us
  transfers between devices with their start and end apart: 2, of which 1 were waited for; matrix products, arithmetic and copies ran while one was open for 1% of the time, Pallas kernels for 2%

profile of v2, /device:TPU:1, one launch (start us, length us, event | category | flops | bytes accessed | tf_op | source)
XLA Modules:
  0.0 110.9 jit_solution(4368076050106837295)
XLA Ops:
  0.6 2.5 %shard_map.77 = (bf16[8,112,512]{2,1,0:T(8,128)(2,1)}, bf16[32,512]{1,0:T(8,128)(2,1)}) custom-call(s32[1,32]{1,0:T(1,128)} %bitcast.3, bf16[1,2,32,4096]{3,2,1,0:T(8,128)(2,1)} %g_ref.1, bf16[1,2,32,256]{3,2,1,0:T(8,128)(2,1)} %l_ref.1), custom_call_target="tpu_custom_call" | custom-call | bytes 1048576 | tf_op jit(solution)/shard_map/pallas_call | solution.py:118
  3.1 7.6 %all-to-all-start = ((bf16[8,112,512]{2,1,0:T(8,128)(2,1)}), bf16[8,112,512]{2,1,0:T(8,128)(2,1)S(1)}, u32[]{:S(2)}, u32[]{:S(2)}) async-start(bf16[8,112,512]{2,1,0:T(8,128)(2,1)} %get-tuple-element.6), calls=%async_computation | async-start | bytes 1835008 | tf_op jit(solution)/shard_map/all_to_all | solution.py:121
  10.8 41.5 %all-gather = bf16[512,512]{1,0:T(8,128)(2,1)} all-gather(bf16[32,512]{1,0:T(8,128)(2,1)} %get-tuple-element.7), channel_id=2, replica_groups=mesh['x'=4,'c'=2,'z'=16,'y'=8] {'z'}, dimensions={0}, use_global_device_ids=true | all-gather | bytes 557056 | tf_op jit(solution)/shard_map/all_gather | solution.py:122
  52.2 0.0 all-to-all-done.b_ref
  52.2 0.0 copy-start
  52.2 0.9 copy-done
  53.2 2.7 %shard_map.78 = (bf16[256,256]{1,0:T(8,128)(2,1)}, bf16[16,16,256]{2,1,0:T(8,128)(2,1)}) custom-call(f32[1,2]{1,0:T(1,128)} %w_ref.3, bf16[8,112,512]{2,1,0:T(8,128)(2,1)} %copy-done, bf16[16,32,512]{2,1,0:T(8,128)(2,1)} %bitcast.2), custom_call_target="tpu_custom_call" | custom-call | flops 536870912 | bytes 1048576 | tf_op jit(solution)/shard_map/pallas_call | solution.py:123
  55.9 3.7 %all-to-all-start.1 = ((bf16[16,16,256]{2,1,0:T(8,128)(2,1)}), bf16[16,16,256]{2,1,0:T(8,128)(2,1)S(1)}, u32[]{:S(2)}, u32[]{:S(2)}) async-start(bf16[16,16,256]{2,1,0:T(8,128)(2,1)} %get-tuple-element.8), calls=%async_computation.1 | async-start | bytes 262144 | tf_op jit(solution)/shard_map/all_to_all | solution.py:126
  59.6 1.4 %slice.4.s_ref = bf16[8,16,128]{2,1,0:T(8,128)(2,1)} slice(bf16[8,112,512]{2,1,0:T(8,128)(2,1)} %copy-done), slice={[0:8], [96:112], [0:128]} | slice | bytes 65536 | tf_op jit(solution)/shard_map/slice | solution.py:129
  61.0 1.8 %shard_map.79.p_ref = bf16[64,8,256]{2,1,0:T(8,128)(2,1)} custom-call(bf16[8,16,128]{2,1,0:T(8,128)(2,1)} %slice.4.s_ref, bf16[256,256]{1,0:T(8,128)(2,1)} %get-tuple-element.9.density_ref), custom_call_target="tpu_custom_call" | custom-call | flops 8388608 | bytes 262144 | tf_op jit(solution)/shard_map/pallas_call | solution.py:127
  62.8 8.8 %all-to-all-done.1.q_ref = bf16[16,16,256]{2,1,0:T(8,128)(2,1)S(1)} async-done(((bf16[16,16,256]{2,1,0:T(8,128)(2,1)}), bf16[16,16,256]{2,1,0:T(8,128)(2,1)S(1)}, u32[]{:S(2)}, u32[]{:S(2)}) %all-to-all-start.1) | async-done | bytes 131104 | tf_op jit(solution)/shard_map/all_to_all | solution.py:126
  71.6 0.0 copy-start.1
  71.7 0.6 copy-done.1
  72.3 1.8 %shard_map.80 = bf16[64,8,384]{2,1,0:T(8,128)(2,1)} custom-call(f32[1,2]{1,0:T(1,128)} %w_ref.3, bf16[16,16,256]{2,1,0:T(8,128)(2,1)} %copy-done.1, bf16[1,2,2,256]{3,2,1,0:T(2,128)(2,1)} %d_ref.1, bf16[64,8,256]{2,1,0:T(8,128)(2,1)} %shard_map.79.p_ref), custom_call_target="tpu_custom_call" | custom-call | bytes 262144 | tf_op jit(solution)/shard_map/pallas_call | solution.py:130
  74.1 33.9 %all_to_all.15.p_ref = bf16[64,8,384]{2,1,0:T(8,128)(2,1)} all-to-all(bf16[64,8,384]{2,1,0:T(8,128)(2,1)} %shard_map.80), channel_id=1, replica_groups=mesh['x'=4,'c'=2,'z'=16,'y'=8] {'x','c','y'}, dimensions={0} | all-to-all | bytes 786432 | tf_op jit(solution)/shard_map/all_to_all | solution.py:133
  108.1 2.8 %shard_map.81 = (f32[2,256]{1,0:T(2,128)}, bf16[8,4096]{1,0:T(8,128)(2,1)}) custom-call(bf16[64,8,384]{2,1,0:T(8,128)(2,1)} %all_to_all.15.p_ref, bf16[256,4096]{1,0:T(8,128)(2,1)} %h_ref.1), custom_call_target="tpu_custom_call" | custom-call | flops 16777216 | bytes 2097152 | tf_op jit(solution)/shard_map/pallas_call | solution.py:134
Async XLA Ops:
  3.1 49.1 %all-to-all-start = ((bf16[8,112,512]{2,1,0:T(8,128)(2,1)}), bf16[8,112,512]{2,1,0:T(8,128)(2,1)S(1)}, u32[]{:S(2)}, u32[]{:S(2)}) async-start(bf16[8,112,512]{2,1,0:T(8,128)(2,1)} %get-tuple-element.6), calls=%async_computation | async-start | bytes 1835008 | tf_op jit(solution)/shard_map/all_to_all | solution.py:121
  52.2 0.9 copy-start
  55.9 15.7 %all-to-all-start.1 = ((bf16[16,16,256]{2,1,0:T(8,128)(2,1)}), bf16[16,16,256]{2,1,0:T(8,128)(2,1)S(1)}, u32[]{:S(2)}, u32[]{:S(2)}) async-start(bf16[16,16,256]{2,1,0:T(8,128)(2,1)} %get-tuple-element.8), calls=%async_computation.1 | async-start | bytes 262144 | tf_op jit(solution)/shard_map/all_to_all | solution.py:126
  71.6 0.6 copy-start.1

commit v3 on v2

--- a/solution.py
+++ b/solution.py
@@ -19,15 +19,24 @@
 SM = pl.BlockSpec(memory_space=pltpu.SMEM)
 
 
-def kernel_call(body, outs, specs, flops=0, moved=0):
-    shapes = tuple(jax.ShapeDtypeStruct(s, d) for s, d in outs)
-    return pl.pallas_call(
+def kernel_call(body, outs, specs, flops=0, moved=0, kept=(True, True)):
+    call = pl.pallas_call(
         body,
-        out_shape=shapes,
+        out_shape=tuple(pltpu.VMEM(s, d) if k else jax.ShapeDtypeStruct(s, d) for (s, d), k in zip(outs, kept)),
         in_specs=specs,
         out_specs=tuple(VM for _ in outs),
         cost_estimate=pl.CostEstimate(flops=flops, bytes_accessed=moved, transcendentals=0),
     )
+
+    def run(*args):
+        return call(
+            *(
+                pltpu.with_memory_space_constraint(arg, pltpu.VMEM) if spec is VM else arg
+                for arg, spec in zip(args, specs, strict=True)
+            )
+        )
+
+    return run
 
 
 def pack_kernel(o_ref, g_ref, l_ref, out_ref, own_ref):
@@ -106,10 +115,9 @@
             out_ref[NY * k + y, :, W:] = tail
 
 
-def energy_kernel(p_ref, h_ref, diag_ref, energy_ref):
+def total_kernel(p_ref, half_ref, diag_ref):
     total = jnp.sum(p_ref[...].astype(F32), axis=0)
-    half = total[:, :W].astype(BF16)
-    energy_ref[...] = jnp.dot(half, h_ref[...], preferred_element_type=F32).astype(BF16)
+    half_ref[...] = total[:, :W].astype(BF16)
     diag_ref[:, 0:128] = total[0:2, W:]
     diag_ref[:, 128:] = total[2:4, W:]
 
@@ -131,9 +139,10 @@
         join_kernel, [((NP * NY, CAP, W + 128), BF16)], [SM, VM, VM, VM], moved=1 << 18
     )(pole_weights, quad, diag_inverse, placed)
     joined = lax.all_to_all(joined, ("x", "c", "y"), 0, 0)
-    density_diag, patch_energy = kernel_call(
-        energy_kernel, [((2, W), F32), ((CAP, NZ * NY * RD), BF16)], [VM, VM], flops=1 << 24, moved=1 << 21
-    )(joined, ham_slab)
+    half, density_diag = kernel_call(
+        total_kernel, [((CAP, W), BF16), ((2, W), F32)], [VM], moved=1 << 18, kept=(True, False)
+    )(joined)
+    patch_energy = jnp.dot(half, ham_slab, preferred_element_type=F32).astype(BF16)
     return (density_diag, patch_energy)
 
 

time: 111 us -> 106 us (0.955)
  Pallas kernels: 11.7 us -> 5.06 us
  blocking collectives: 75.4 us -> 70.8 us
  waiting for transfers between devices: 8.83 us -> 11.7 us
  starting transfers between devices: 11.3 us -> 13.3 us
    pallas_call x5, Pallas kernels: 11.7 us -> 5.06 us  [run(): call(*(pltpu.with_memory_space_constraint(arg, pltpu.VMEM) if spec is VM...]
    all_to_all x1, waiting for transfers between devices: 8.83 us -> 11.7 us  [per_device(): quad = lax.all_to_all(quad, 'z', 0, 0)]
    all_to_all x1, blocking collectives: 33.9 us -> 31.4 us  [per_device(): joined = lax.all_to_all(joined, ('x', 'c', 'y'), 0, 0)]
    all_gather x1, blocking collectives: 41.5 us -> 39.4 us  [per_device(): columns = lax.all_gather(own, 'z')]
    all_to_all x1, starting transfers between devices: 3.67 us -> 5.71 us  [per_device(): quad = lax.all_to_all(quad, 'z', 0, 0)]
    slice x1, local copies, waits for them, and re-layouts: 1.38 us -> 0.01 us  [per_device(): block[:, 3 * RD:, :128]]
    unnamed x4 -> x10, local copies, waits for them, and re-layouts: 1.6 us -> 2.45 us
  transfers between devices with their start and end apart: 2 -> 2, of which waited for: 1 -> 1; matrix products, arithmetic and copies ran while one was open for 1% -> 0% of each run, Pallas kernels for 2% -> 0%
where the time goes in v3:
time: 106 us; the launch traced here: 105 us
  blocking collectives  70.8 us (67%)
  starting transfers between devices  13.3 us (13%)
  waiting for transfers between devices  11.7 us (11%)
  Pallas kernels  5.06 us (5%)
  local copies, waits for them, and re-layouts  2.46 us (2%)
    all_gather x1, blocking collectives, per_device(): columns = lax.all_gather(own, 'z')  39.4 us
    all_to_all x1, blocking collectives, per_device(): joined = lax.all_to_all(joined, ('x', 'c', 'y'), 0, 0)  31.4 us
    all_to_all x1, waiting for transfers between devices, per_device(): quad = lax.all_to_all(quad, 'z', 0, 0)  11.7 us
    all_to_all x1, starting transfers between devices, per_device(): block = lax.all_to_all(packed, 'y', 0, 0)  7.64 us
    all_to_all x1, starting transfers between devices, per_device(): quad = lax.all_to_all(quad, 'z', 0, 0)  5.71 us
    pallas_call x5, Pallas kernels, run(): call(*(pltpu.with_memory_space_constraint(arg, pltpu.VMEM) if spec is VM...  5.06 us
    unnamed x10, local copies, waits for them, and re-layouts  2.45 us
  transfers between devices with their start and end apart: 2, of which 1 were waited for; matrix products, arithmetic and copies ran while one was open for 0% of the time, Pallas kernels for 0%

profile of v3, /device:TPU:1, one launch (start us, length us, event | category | flops | bytes accessed | tf_op | source)
XLA Modules:
  0.0 105.1 jit_solution(12873304653407439135)
XLA Ops:
  0.6 0.0 copy-start
  0.6 1.0 copy-done
  1.7 0.0 copy-start.1
  1.7 0.8 copy-done.1
  2.4 0.0 copy-start.3
  2.4 0.7 copy-done.3
  3.1 1.4 %shard_map.77 = (bf16[8,112,512]{2,1,0:T(8,128)(2,1)}, bf16[32,512]{1,0:T(8,128)(2,1)S(1)}) custom-call(s32[1,32]{1,0:T(1,128)S(1)} %bitcast.5, bf16[1,2,32,4096]{3,2,1,0:T(8,128)(2,1)S(1)} %copy-done, bf16[1,2,32,256]{3,2,1,0:T(8,128)(2,1)S(1)} %copy-done.1), custom_call_target="tpu_custom_call" | custom-call | bytes 1048576 | tf_op jit(solution)/shard_map/pallas_call | solution.py:32
  4.5 7.6 %all-to-all-start = ((bf16[8,112,512]{2,1,0:T(8,128)(2,1)}), bf16[8,112,512]{2,1,0:T(8,128)(2,1)S(1)}, u32[]{:S(2)}, u32[]{:S(2)}) async-start(bf16[8,112,512]{2,1,0:T(8,128)(2,1)} %get-tuple-element.8), calls=%async_computation | async-start | bytes 1835008 | tf_op jit(solution)/shard_map/all_to_all | solution.py:129
  12.2 0.0 copy-start.2
  12.2 39.4 %all-gather = bf16[512,512]{1,0:T(8,128)(2,1)S(1)} all-gather(bf16[32,512]{1,0:T(8,128)(2,1)S(1)} %get-tuple-element.9), channel_id=2, replica_groups=mesh['x'=4,'c'=2,'z'=16,'y'=8] {'z'}, dimensions={0}, use_global_device_ids=true | all-gather | bytes 557056 | tf_op jit(solution)/shard_map/all_gather | solution.py:130
  51.6 0.0 all-to-all-done.b_ref
  51.6 2.1 %shard_map.78 = (bf16[256,256]{1,0:T(8,128)(2,1)S(1)}, bf16[16,16,256]{2,1,0:T(8,128)(2,1)}) custom-call(f32[1,2]{1,0:T(1,128)} %w_ref.3, bf16[8,112,512]{2,1,0:T(8,128)(2,1)S(1)} %all-to-all-done.b_ref, bf16[16,32,512]{2,1,0:T(8,128)(2,1)S(1)} %bitcast.4), custom_call_target="tpu_custom_call" | custom-call | flops 536870912 | bytes 1048576 | tf_op jit(solution)/shard_map/pallas_call | solution.py:32
  53.6 0.0 copy-start.4
  53.6 5.7 %all-to-all-start.1 = ((bf16[16,16,256]{2,1,0:T(8,128)(2,1)}), bf16[16,16,256]{2,1,0:T(8,128)(2,1)S(1)}, u32[]{:S(2)}, u32[]{:S(2)}) async-start(bf16[16,16,256]{2,1,0:T(8,128)(2,1)} %get-tuple-element.10), calls=%async_computation.1 | async-start | bytes 262144 | tf_op jit(solution)/shard_map/all_to_all | solution.py:134
  59.3 0.2 shard_map.79.p_ref
  59.6 11.7 %all-to-all-done.1.q_ref = bf16[16,16,256]{2,1,0:T(8,128)(2,1)S(1)} async-done(((bf16[16,16,256]{2,1,0:T(8,128)(2,1)}), bf16[16,16,256]{2,1,0:T(8,128)(2,1)S(1)}, u32[]{:S(2)}, u32[]{:S(2)}) %all-to-all-start.1) | async-done | bytes 131104 | tf_op jit(solution)/shard_map/all_to_all | solution.py:134
  71.3 0.0 copy-done.2
  71.3 0.7 shard_map.80
  72.0 31.4 %all_to_all.15.p_ref = bf16[64,8,384]{2,1,0:T(8,128)(2,1)S(1)} all-to-all(bf16[64,8,384]{2,1,0:T(8,128)(2,1)S(1)} %shard_map.80), channel_id=1, replica_groups=mesh['x'=4,'c'=2,'z'=16,'y'=8] {'x','c','y'}, dimensions={0} | all-to-all | bytes 786432 | tf_op jit(solution)/shard_map/all_to_all | solution.py:141
  103.4 0.6 shard_map.81
  104.0 0.0 copy-done.4
  104.0 1.0 convolution_convert_fusion
  (1 shorter events, 0.0 us)
Async XLA Ops:
  0.6 1.0 copy-start
  1.7 0.8 copy-start.1
  2.4 0.7 copy-start.3
  4.5 47.0 %all-to-all-start = ((bf16[8,112,512]{2,1,0:T(8,128)(2,1)}), bf16[8,112,512]{2,1,0:T(8,128)(2,1)S(1)}, u32[]{:S(2)}, u32[]{:S(2)}) async-start(bf16[8,112,512]{2,1,0:T(8,128)(2,1)} %get-tuple-element.8), calls=%async_computation | async-start | bytes 1835008 | tf_op jit(solution)/shard_map/all_to_all | solution.py:129
  12.2 59.1 %copy-start.2 = (bf16[1,2,2,256]{3,2,1,0:T(2,128)(2,1)S(1)}, bf16[1,2,2,256]{3,2,1,0:T(2,128)(2,1)}, u32[]{:S(2)}) copy-start(bf16[1,2,2,256]{3,2,1,0:T(2,128)(2,1)} %d_ref.1) | copy-start | bytes 6148
  53.6 50.4 %copy-start.4 = (bf16[256,4096]{1,0:T(8,128)(2,1)S(1)}, bf16[256,4096]{1,0:T(8,128)(2,1)}, u32[]{:S(2)}) copy-start(bf16[256,4096]{1,0:T(8,128)(2,1)} %param.11) | copy-start | bytes 6291460
  53.6 17.7 %all-to-all-start.1 = ((bf16[16,16,256]{2,1,0:T(8,128)(2,1)}), bf16[16,16,256]{2,1,0:T(8,128)(2,1)S(1)}, u32[]{:S(2)}, u32[]{:S(2)}) async-start(bf16[16,16,256]{2,1,0:T(8,128)(2,1)} %get-tuple-element.10), calls=%async_computation.1 | async-start | bytes 262144 | tf_op jit(solution)/shard_map/all_to_all | solution.py:134

commit v4 on v3

--- a/solution.py
+++ b/solution.py
@@ -6,7 +6,6 @@
 from jax.sharding import Mesh, PartitionSpec as P
 
 NX, NC, NZ, NY = 4, 2, 16, 8
-NP = NX * NC
 RD = 32
 W = 256
 ZR = NY * RD
@@ -39,24 +38,40 @@
     return run
 
 
-def pack_kernel(o_ref, g_ref, l_ref, out_ref, own_ref):
-    owner = jnp.broadcast_to(o_ref[...], (RD, RD))
-    row = lax.broadcasted_iota(jnp.int32, (RD, RD), 0)
-    column = lax.broadcasted_iota(jnp.int32, (RD, RD), 1)
-    owner_down = jnp.sum(jnp.where(row == column, owner, 0), axis=1, keepdims=True)
-    earlier = (owner_down == owner) & (row < column)
-    rank = jnp.sum(earlier.astype(jnp.int32), axis=0, keepdims=True)
-    slot = (o_ref[...] * CAP + rank).astype(F32)
-    slot = jnp.broadcast_to(slot, (TAIL, RD)).astype(BF16)
-    for y in range(NY):
-        out_ref[y, 3 * RD :, :] = jnp.zeros((TAIL, YC), BF16)
-        out_ref[y, 3 * RD :, 0:RD] = slot
+def pack_kernel(o_hbm, g_hbm, l_hbm, out_hbm, own_ref, o_ref, g_ref, l_ref, out_ref, in_sem, out_sem):
+    owners_in = pltpu.make_async_copy(o_hbm, o_ref, in_sem.at[0])
+    rows_in = pltpu.make_async_copy(l_hbm, l_ref, in_sem.at[1])
+    wide = NZ * W // 2
+    pieces_in = [
+        [
+            pltpu.make_async_copy(
+                g_hbm.at[0, part, :, pl.ds(wide * side, wide)],
+                g_ref.at[part, :, pl.ds(wide * side, wide)],
+                in_sem.at[2 + 2 * part + side],
+            )
+            for side in range(2)
+        ]
+        for part in range(2)
+    ]
+    pieces_out = [
+        pltpu.make_async_copy(
+            out_ref.at[:, pl.ds(start, size), :], out_hbm.at[:, pl.ds(start, size), :], out_sem.at[i]
+        )
+        for i, (start, size) in enumerate(((0, RD), (RD, RD), (2 * RD, RD + TAIL)))
+    ]
+    for part in range(2):
+        for side in range(2):
+            pieces_in[part][side].start()
+    owners_in.start()
+    rows_in.start()
     quarter = lax.broadcasted_iota(jnp.int32, (RD, 128), 1) // 32
     for part in range(2):
-        for half in range(2):
-            for tile in range(4):
+        for tile in range(4):
+            if tile % 2 == 0:
+                pieces_in[part][tile // 2].wait()
+            for half in range(2):
                 loaded = [
-                    g_ref[0, part, :, (4 * tile + j) * W + half * 128 : (4 * tile + j) * W + half * 128 + 128].astype(F32)
+                    g_ref[part, :, (4 * tile + j) * W + half * 128 : (4 * tile + j) * W + half * 128 + 128].astype(F32)
                     for j in range(4)
                 ]
                 for q in range(4):
@@ -66,11 +81,50 @@
                         moved = pltpu.roll(loaded[j], shift, 1) if shift else loaded[j]
                         joined = moved if joined is None else jnp.where(quarter == j, moved, joined)
                     out_ref[4 * half + q, RD * part : RD * part + RD, 128 * tile : 128 * tile + 128] = joined.astype(BF16)
-    for part in range(2):
-        rows = l_ref[0, part]
-        own_ref[:, W * part : W * part + W] = rows
-        for y in range(NY):
-            out_ref[y, 2 * RD : 3 * RD, W * part : W * part + W] = rows
+        pieces_out[part].start()
+        if part == 0:
+            owners_in.wait()
+            rows_in.wait()
+            owner = jnp.broadcast_to(o_ref[...], (RD, RD))
+            row = lax.broadcasted_iota(jnp.int32, (RD, RD), 0)
+            column = lax.broadcasted_iota(jnp.int32, (RD, RD), 1)
+            owner_down = jnp.sum(jnp.where(row == column, owner, 0), axis=1, keepdims=True)
+            earlier = (owner_down == owner) & (row < column)
+            rank = jnp.sum(earlier.astype(jnp.int32), axis=0, keepdims=True)
+            slot = (o_ref[...] * CAP + rank).astype(F32)
+            slot = jnp.broadcast_to(slot, (TAIL, RD)).astype(BF16)
+            for y in range(NY):
+                out_ref[y, 3 * RD :, :] = jnp.zeros((TAIL, YC), BF16)
+                out_ref[y, 3 * RD :, 0:RD] = slot
+            for side in range(2):
+                rows = l_ref[0, side]
+                own_ref[:, W * side : W * side + W] = rows
+                for y in range(NY):
+                    out_ref[y, 2 * RD : 3 * RD, W * side : W * side + W] = rows
+            pieces_out[2].start()
+    for piece in pieces_out:
+        piece.wait()
+
+
+def pack(owner_map, trailing, panel):
+    packed = (NY, 3 * RD + TAIL, YC)
+    anywhere = pl.BlockSpec(memory_space=pl.ANY)
+    return pl.pallas_call(
+        pack_kernel,
+        out_shape=(jax.ShapeDtypeStruct(packed, BF16), pltpu.VMEM((RD, 2 * W), BF16)),
+        in_specs=[anywhere] * 3,
+        out_specs=(anywhere, VM),
+        scratch_shapes=[
+            pltpu.VMEM((1, RD), jnp.int32),
+            pltpu.VMEM((2, RD, NZ * W), BF16),
+            pltpu.VMEM((1, 2, RD, W), BF16),
+            pltpu.VMEM(packed, BF16),
+            pltpu.SemaphoreType.DMA((6,)),
+            pltpu.SemaphoreType.DMA((3,)),
+        ],
+        name="pack",
+        cost_estimate=pl.CostEstimate(flops=0, bytes_accessed=1 << 20, transcendentals=0),
+    )(owner_map.reshape(1, RD), trailing, panel)
 
 
 def cross_kernel(w_ref, b_ref, l_ref, density_ref, quad_ref):
@@ -91,28 +145,34 @@
     density_ref[...] = (-even).astype(BF16)
 
 
-def place_kernel(s_ref, density_ref, out_ref):
-    index = lax.broadcasted_iota(jnp.int32, (NP * CAP, RD), 0)
+def place_kernel(s_ref, density_ref, mine_ref, other_ref):
+    core = lax.axis_index("c")
+    line = lax.broadcasted_iota(jnp.int32, (2 * NX * CAP, RD), 0)
+    half = line // (NX * CAP)
+    within = line % (NX * CAP)
+    side = jnp.where(half == 0, core, 1 - core)
+    index = (within // CAP * NC + side) * CAP + within % CAP
     for y in range(NY):
         slot = s_ref[y, 0:1, 0:RD].astype(F32).astype(jnp.int32)
         place = (index == slot).astype(F32).astype(BF16)
         rows = density_ref[RD * y : RD * y + RD, :]
         placed = jnp.dot(place, rows, preferred_element_type=F32).astype(BF16)
-        for k in range(NP):
-            out_ref[NY * k + y] = placed[CAP * k : CAP * k + CAP]
-
-
-def join_kernel(w_ref, q_ref, d_ref, p_ref, out_ref):
+        for x in range(NX):
+            mine_ref[NY * x + y] = placed[CAP * x : CAP * x + CAP]
+            other_ref[NY * x + y] = placed[CAP * (NX + x) : CAP * (NX + x) + CAP]
+
+
+def join_kernel(w_ref, q_ref, d_ref, p_ref, o_ref, out_ref):
     quad = jnp.sum(q_ref[...].astype(F32), axis=0)
     diag = w_ref[0, 0] * d_ref[0, 1].astype(F32) + w_ref[0, 1] * d_ref[0, 0].astype(F32)
     here = lax.axis_index("y")
     zero = jnp.zeros((CAP - 4, 128), F32)
+    out_ref[:, :, 0:W] = (p_ref[...].astype(F32) + o_ref[...].astype(F32)).astype(BF16)
     for y in range(NY):
         rows = quad[2 * y : 2 * y + 2] + jnp.where(here == y, diag, 0.0)
         tail = jnp.concatenate([rows[:, :128], rows[:, 128:], zero], axis=0).astype(BF16)
-        for k in range(NP):
-            out_ref[NY * k + y, :, 0:W] = p_ref[NY * k + y]
-            out_ref[NY * k + y, :, W:] = tail
+        for x in range(NX):
+            out_ref[NY * x + y, :, W:] = tail
 
 
 def total_kernel(p_ref, half_ref, diag_ref):
@@ -123,25 +183,24 @@
 
 
 def per_device(trailing, panel, diag_inverse, pole_weights, owner_map, ham_slab):
-    packed, own = kernel_call(
-        pack_kernel, [((NY, 3 * RD + TAIL, YC), BF16), ((RD, 2 * W), BF16)], [VM] * 3, moved=1 << 20
-    )(owner_map.reshape(1, RD), trailing, panel)
+    packed, own = pack(owner_map, trailing, panel)
     block = lax.all_to_all(packed, "y", 0, 0)
     columns = lax.all_gather(own, "z")
     density, quad = kernel_call(
         cross_kernel, [((ZR, W), BF16), ((NZ, W // NZ, W), BF16)], [SM, VM, VM], flops=1 << 29, moved=1 << 20
     )(pole_weights, block, columns)
     quad = lax.all_to_all(quad, "z", 0, 0)
-    (placed,) = kernel_call(
-        place_kernel, [((NP * NY, CAP, W), BF16)], [VM, VM], flops=1 << 23, moved=1 << 18
+    mine, other = kernel_call(
+        place_kernel, [((NX * NY, CAP, W), BF16)] * 2, [VM, VM], flops=1 << 23, moved=1 << 18
     )(block[:, 3 * RD :, :128], density)
+    swap = ((0, 1), (1, 0))
+    other = lax.ppermute(other, "c", swap)
     (joined,) = kernel_call(
-        join_kernel, [((NP * NY, CAP, W + 128), BF16)], [SM, VM, VM, VM], moved=1 << 18
-    )(pole_weights, quad, diag_inverse, placed)
-    joined = lax.all_to_all(joined, ("x", "c", "y"), 0, 0)
-    half, density_diag = kernel_call(
-        total_kernel, [((CAP, W), BF16), ((2, W), F32)], [VM], moved=1 << 18, kept=(True, False)
-    )(joined)
+        join_kernel, [((NX * NY, CAP, W + 128), BF16)], [SM, VM, VM, VM, VM], moved=1 << 18
+    )(pole_weights, quad, diag_inverse, mine, other)
+    joined = lax.all_to_all(joined, ("x", "y"), 0, 0)
+    half, diag = kernel_call(total_kernel, [((CAP, W), BF16), ((2, W), F32)], [VM], moved=1 << 18)(joined)
+    density_diag = diag + lax.ppermute(diag, "c", swap)
     patch_energy = jnp.dot(half, ham_slab, preferred_element_type=F32).astype(BF16)
     return (density_diag, patch_energy)
 

time: 106 us -> 103 us (0.972)
  starting transfers between devices: 13.3 us -> 31.8 us
  blocking collectives: 70.8 us -> 56.6 us
  waiting for transfers between devices: 11.7 us -> 4.7 us
  local copies, waits for them, and re-layouts: 2.46 us -> 0.01 us
  matrix products: 1.02 us -> 2.61 us
    ppermute x0 -> x2, starting transfers between devices: none -> 18.6 us  [the longest x1 11.6 us: per_device(): density_diag = diag + lax.ppermute(diag, 'c', swap)]
    all_to_all x1, blocking collectives: 31.4 us -> 17.3 us  [per_device(): joined = lax.all_to_all(joined, ('x', 'y'), 0, 0)]
    all_to_all x1, waiting for transfers between devices: 11.7 us -> 3.73 us  [per_device(): quad = lax.all_to_all(quad, 'z', 0, 0)]
    pallas_call x0 -> x1, Pallas kernels: none -> 2.52 us  [pack(): pl.pallas_call(pack_kernel, out_shape=(jax.ShapeDtypeStruct(packed, BF16)...]
    unnamed x10 -> x2, local copies, waits for them, and re-layouts: 2.45 us -> 0.01 us
    pallas_call x5 -> x4, Pallas kernels: 5.06 us -> 3.06 us  [run(): call(*(pltpu.with_memory_space_constraint(arg, pltpu.VMEM) if spec is VM...]
    dot_general x1, matrix products: 1.02 us -> 2.61 us  [per_device(): jnp.dot(half, ham_slab, preferred_element_type=F32).astype(BF16)]
  transfers between devices with their start and end apart: 2 -> 4, of which waited for: 1 -> 2; matrix products, arithmetic and copies ran while one was open for 0% -> 3% of each run, Pallas kernels for 0% -> 0%
where the time goes in v4:
time: 103 us
  blocking collectives  56.6 us (55%)
  starting transfers between devices  31.8 us (31%)
  Pallas kernels  5.58 us (5%)
  waiting for transfers between devices  4.7 us (5%)
  matrix products  2.61 us (3%)
    all_gather x1, blocking collectives, per_device(): columns = lax.all_gather(own, 'z')  39.4 us
    all_to_all x1, blocking collectives, per_device(): joined = lax.all_to_all(joined, ('x', 'y'), 0, 0)  17.3 us
    ppermute x1, starting transfers between devices, per_device(): density_diag = diag + lax.ppermute(diag, 'c', swap)  11.6 us
    all_to_all x1, starting transfers between devices, per_device(): block = lax.all_to_all(packed, 'y', 0, 0)  7.65 us
    ppermute x1, starting transfers between devices, per_device(): other = lax.ppermute(other, 'c', swap)  7.02 us
    all_to_all x1, starting transfers between devices, per_device(): quad = lax.all_to_all(quad, 'z', 0, 0)  5.59 us
    all_to_all x1, waiting for transfers between devices, per_device(): quad = lax.all_to_all(quad, 'z', 0, 0)  3.73 us
    pallas_call x4, Pallas kernels, run(): call(*(pltpu.with_memory_space_constraint(arg, pltpu.VMEM) if spec is VM...  3.06 us
  transfers between devices with their start and end apart: 4, of which 2 were waited for; matrix products, arithmetic and copies ran while one was open for 3% of the time, Pallas kernels for 0%

profile of v4, /device:TPU:1, one launch (start us, length us, event | category | flops | bytes accessed | tf_op | source)
XLA Modules:
  0.0 102.6 jit_solution(8391901674224407078)
XLA Ops:
  0.6 2.5 %pack.1 = (bf16[8,112,512]{2,1,0:T(8,128)(2,1)}, bf16[32,512]{1,0:T(8,128)(2,1)S(1)}) custom-call(s32[1,32]{1,0:T(1,128)} %bitcast.5, bf16[1,2,32,4096]{3,2,1,0:T(8,128)(2,1)} %g_hbm.1, bf16[1,2,32,256]{3,2,1,0:T(8,128)(2,1)} %l_hbm.1), custom_call_target="tpu_custom_call" | custom-call | bytes 1048576 | tf_op jit(solution)/shard_map/pack/pallas_call | solution.py:112
  3.2 0.0 copy-start
  3.2 7.7 %all-to-all-start = ((bf16[8,112,512]{2,1,0:T(8,128)(2,1)}), bf16[8,112,512]{2,1,0:T(8,128)(2,1)S(1)}, u32[]{:S(2)}, u32[]{:S(2)}) async-start(bf16[8,112,512]{2,1,0:T(8,128)(2,1)} %get-tuple-element.10), calls=%async_computation | async-start | bytes 1835008 | tf_op jit(solution)/shard_map/all_to_all | solution.py:187
  10.8 39.4 %all-gather = bf16[512,512]{1,0:T(8,128)(2,1)S(1)} all-gather(bf16[32,512]{1,0:T(8,128)(2,1)S(1)} %get-tuple-element.11), channel_id=2, replica_groups=mesh['x'=4,'c'=2,'z'=16,'y'=8] {'z'}, dimensions={0}, use_global_device_ids=true | all-gather | bytes 557056 | tf_op jit(solution)/shard_map/all_gather | solution.py:188
  50.2 0.0 all-to-all-done.b_ref
  50.2 2.1 %shard_map.77 = (bf16[256,256]{1,0:T(8,128)(2,1)S(1)}, bf16[16,16,256]{2,1,0:T(8,128)(2,1)}) custom-call(f32[1,2]{1,0:T(1,128)} %w_ref.3, bf16[8,112,512]{2,1,0:T(8,128)(2,1)S(1)} %all-to-all-done.b_ref, bf16[16,32,512]{2,1,0:T(8,128)(2,1)S(1)} %bitcast.4), custom_call_target="tpu_custom_call" | custom-call | flops 536870912 | bytes 1048576 | tf_op jit(solution)/shard_map/pallas_call | solution.py:31
  52.3 5.6 %all-to-all-start.1 = ((bf16[16,16,256]{2,1,0:T(8,128)(2,1)}), bf16[16,16,256]{2,1,0:T(8,128)(2,1)S(1)}, u32[]{:S(2)}, u32[]{:S(2)}) async-start(bf16[16,16,256]{2,1,0:T(8,128)(2,1)} %get-tuple-element.12), calls=%async_computation.1 | async-start | bytes 262144 | tf_op jit(solution)/shard_map/all_to_all | solution.py:192
  57.9 0.2 shard_map.78
  58.1 7.0 %collective-permute-start = (bf16[32,8,256]{2,1,0:T(8,128)(2,1)S(1)}, bf16[32,8,256]{2,1,0:T(8,128)(2,1)S(1)}, u32[]{:S(2)}, u32[]{:S(2)}) collective-permute-start(bf16[32,8,256]{2,1,0:T(8,128)(2,1)S(1)} %get-tuple-element.15), channel_id=1, source_target_pairs={{0,128},{128,0},{1,129},{129,1},{2,130},{130,2},{3,131},{131,3},{4... | collective-permute-start | bytes 393224 | tf_op jit(solution)/shard_map/ppermute | solution.py:197
  65.1 1.0 collective-permute-done.o_ref
  66.1 3.7 %all-to-all-done.1.q_ref = bf16[16,16,256]{2,1,0:T(8,128)(2,1)S(1)} async-done(((bf16[16,16,256]{2,1,0:T(8,128)(2,1)}), bf16[16,16,256]{2,1,0:T(8,128)(2,1)S(1)}, u32[]{:S(2)}, u32[]{:S(2)}) %all-to-all-start.1) | async-done | bytes 131104 | tf_op jit(solution)/shard_map/all_to_all | solution.py:192
  69.8 0.0 copy-done
  69.8 0.7 shard_map.79
  70.6 17.3 %all_to_all.15.p_ref = bf16[32,8,384]{2,1,0:T(8,128)(2,1)S(1)} all-to-all(bf16[32,8,384]{2,1,0:T(8,128)(2,1)S(1)} %shard_map.79), channel_id=1, replica_groups=mesh['x'=4,'c'=2,'z'=16,'y'=8] {'x','y'}, dimensions={0} | all-to-all | bytes 393216 | tf_op jit(solution)/shard_map/all_to_all | solution.py:201
  87.9 11.6 %collective-permute-start.1 = (f32[2,256]{1,0:T(2,128)S(1)}, f32[2,256]{1,0:T(2,128)S(1)}, u32[]{:S(2)}, u32[]{:S(2)}) collective-permute-start(f32[2,256]{1,0:T(2,128)S(1)} %get-tuple-element.16), channel_id=1, source_target_pairs={{0,128},{128,0},{1,129},{129,1},{2,130},{130,2},{3,131},{131,3},{4... | collective-permute-start | bytes 6152 | tf_op jit(solution)/shard_map/ppermute | solution.py:203
  99.5 2.6 %convolution_convert_fusion = bf16[8,4096]{1,0:T(8,128)(2,1)} fusion(bf16[8,256]{1,0:T(8,128)(2,1)S(1)} %get-tuple-element.17, bf16[256,4096]{1,0:T(8,128)(2,1)} %param.11), kind=kOutput, calls=%fused_computation | convolution fusion | flops 16809984 | bytes 2166784 | tf_op jit(solution)/shard_map/dot_general | solution.py:204
  102.1 0.0 collective-permute-done.1
  102.1 0.6 add.3
  (2 shorter events, 0.0 us)
Async XLA Ops:
  3.2 66.7 %copy-start = (bf16[1,2,2,256]{3,2,1,0:T(2,128)(2,1)S(1)}, bf16[1,2,2,256]{3,2,1,0:T(2,128)(2,1)}, u32[]{:S(2)}) copy-start(bf16[1,2,2,256]{3,2,1,0:T(2,128)(2,1)} %d_ref.1) | copy-start | bytes 6148
  3.2 47.0 %all-to-all-start = ((bf16[8,112,512]{2,1,0:T(8,128)(2,1)}), bf16[8,112,512]{2,1,0:T(8,128)(2,1)S(1)}, u32[]{:S(2)}, u32[]{:S(2)}) async-start(bf16[8,112,512]{2,1,0:T(8,128)(2,1)} %get-tuple-element.10), calls=%async_computation | async-start | bytes 1835008 | tf_op jit(solution)/shard_map/all_to_all | solution.py:187
  52.3 17.6 %all-to-all-start.1 = ((bf16[16,16,256]{2,1,0:T(8,128)(2,1)}), bf16[16,16,256]{2,1,0:T(8,128)(2,1)S(1)}, u32[]{:S(2)}, u32[]{:S(2)}) async-start(bf16[16,16,256]{2,1,0:T(8,128)(2,1)} %get-tuple-element.12), calls=%async_computation.1 | async-start | bytes 262144 | tf_op jit(solution)/shard_map/all_to_all | solution.py:192
  58.1 8.0 %collective-permute-start = (bf16[32,8,256]{2,1,0:T(8,128)(2,1)S(1)}, bf16[32,8,256]{2,1,0:T(8,128)(2,1)S(1)}, u32[]{:S(2)}, u32[]{:S(2)}) collective-permute-start(bf16[32,8,256]{2,1,0:T(8,128)(2,1)S(1)} %get-tuple-element.15), channel_id=1, source_target_pairs={{0,128},{128,0},{1,129},{129,1},{2,130},{130,2},{3,131},{131,3},{4... | collective-permute-start | bytes 393224 | tf_op jit(solution)/shard_map/ppermute | solution.py:197
  87.9 14.2 %collective-permute-start.1 = (f32[2,256]{1,0:T(2,128)S(1)}, f32[2,256]{1,0:T(2,128)S(1)}, u32[]{:S(2)}, u32[]{:S(2)}) collective-permute-start(f32[2,256]{1,0:T(2,128)S(1)} %get-tuple-element.16), channel_id=1, source_target_pairs={{0,128},{128,0},{1,129},{129,1},{2,130},{130,2},{3,131},{131,3},{4... | collective-permute-start | bytes 6152 | tf_op jit(solution)/shard_map/ppermute | solution.py:203

commit v5 on v4

--- a/solution.py
+++ b/solution.py
@@ -12,18 +12,20 @@
 YC = NZ * RD
 CAP = 8
 TAIL = 16
+PIECE = 1024
 F32 = jnp.float32
 BF16 = jnp.bfloat16
 VM = pl.BlockSpec(memory_space=pltpu.VMEM)
 SM = pl.BlockSpec(memory_space=pltpu.SMEM)
 
 
-def kernel_call(body, outs, specs, flops=0, moved=0, kept=(True, True)):
+def kernel_call(body, outs, specs, flops=0, moved=0, kept=(True, True), scratch=()):
     call = pl.pallas_call(
         body,
         out_shape=tuple(pltpu.VMEM(s, d) if k else jax.ShapeDtypeStruct(s, d) for (s, d), k in zip(outs, kept)),
         in_specs=specs,
         out_specs=tuple(VM for _ in outs),
+        scratch_shapes=scratch,
         cost_estimate=pl.CostEstimate(flops=flops, bytes_accessed=moved, transcendentals=0),
     )
 
@@ -53,17 +55,39 @@
         ]
         for part in range(2)
     ]
+    spans = [(RD * part, RD, 256 * side, 256) for part in range(2) for side in range(2)] + [(2 * RD, RD + TAIL, 0, YC)]
     pieces_out = [
         pltpu.make_async_copy(
-            out_ref.at[:, pl.ds(start, size), :], out_hbm.at[:, pl.ds(start, size), :], out_sem.at[i]
+            out_ref.at[:, pl.ds(row, rows), pl.ds(lane, lanes)],
+            out_hbm.at[:, pl.ds(row, rows), pl.ds(lane, lanes)],
+            out_sem.at[i],
         )
-        for i, (start, size) in enumerate(((0, RD), (RD, RD), (2 * RD, RD + TAIL)))
+        for i, (row, rows, lane, lanes) in enumerate(spans)
     ]
+    owners_in.start()
+    rows_in.start()
     for part in range(2):
         for side in range(2):
             pieces_in[part][side].start()
-    owners_in.start()
-    rows_in.start()
+    rows_in.wait()
+    for side in range(2):
+        rows = l_ref[0, side]
+        own_ref[:, W * side : W * side + W] = rows
+        for y in range(NY):
+            out_ref[y, 2 * RD : 3 * RD, W * side : W * side + W] = rows
+    owners_in.wait()
+    owner = jnp.broadcast_to(o_ref[...], (RD, RD))
+    row = lax.broadcasted_iota(jnp.int32, (RD, RD), 0)
+    column = lax.broadcasted_iota(jnp.int32, (RD, RD), 1)
+    owner_down = jnp.sum(jnp.where(row == column, owner, 0), axis=1, keepdims=True)
+    earlier = (owner_down == owner) & (row < column)
+    rank = jnp.sum(earlier.astype(jnp.int32), axis=0, keepdims=True)
+    slot = (o_ref[...] * CAP + rank).astype(F32)
+    slot = jnp.broadcast_to(slot, (TAIL, RD)).astype(BF16)
+    for y in range(NY):
+        out_ref[y, 3 * RD :, :] = jnp.zeros((TAIL, YC), BF16)
+        out_ref[y, 3 * RD :, 0:RD] = slot
+    pieces_out[4].start()
     quarter = lax.broadcasted_iota(jnp.int32, (RD, 128), 1) // 32
     for part in range(2):
         for tile in range(4):
@@ -81,27 +105,8 @@
                         moved = pltpu.roll(loaded[j], shift, 1) if shift else loaded[j]
                         joined = moved if joined is None else jnp.where(quarter == j, moved, joined)
                     out_ref[4 * half + q, RD * part : RD * part + RD, 128 * tile : 128 * tile + 128] = joined.astype(BF16)
-        pieces_out[part].start()
-        if part == 0:
-            owners_in.wait()
-            rows_in.wait()
-            owner = jnp.broadcast_to(o_ref[...], (RD, RD))
-            row = lax.broadcasted_iota(jnp.int32, (RD, RD), 0)
-            column = lax.broadcasted_iota(jnp.int32, (RD, RD), 1)
-            owner_down = jnp.sum(jnp.where(row == column, owner, 0), axis=1, keepdims=True)
-            earlier = (owner_down == owner) & (row < column)
-            rank = jnp.sum(earlier.astype(jnp.int32), axis=0, keepdims=True)
-            slot = (o_ref[...] * CAP + rank).astype(F32)
-            slot = jnp.broadcast_to(slot, (TAIL, RD)).astype(BF16)
-            for y in range(NY):
-                out_ref[y, 3 * RD :, :] = jnp.zeros((TAIL, YC), BF16)
-                out_ref[y, 3 * RD :, 0:RD] = slot
-            for side in range(2):
-                rows = l_ref[0, side]
-                own_ref[:, W * side : W * side + W] = rows
-                for y in range(NY):
-                    out_ref[y, 2 * RD : 3 * RD, W * side : W * side + W] = rows
-            pieces_out[2].start()
+            if tile % 2 == 1:
+                pieces_out[2 * part + tile // 2].start()
     for piece in pieces_out:
         piece.wait()
 
@@ -120,7 +125,7 @@
             pltpu.VMEM((1, 2, RD, W), BF16),
             pltpu.VMEM(packed, BF16),
             pltpu.SemaphoreType.DMA((6,)),
-            pltpu.SemaphoreType.DMA((3,)),
+            pltpu.SemaphoreType.DMA((5,)),
         ],
         name="pack",
         cost_estimate=pl.CostEstimate(flops=0, bytes_accessed=1 << 20, transcendentals=0),
@@ -175,11 +180,18 @@
             out_ref[NY * x + y, :, W:] = tail
 
 
-def total_kernel(p_ref, half_ref, diag_ref):
+def total_kernel(p_ref, h_hbm, diag_ref, energy_ref, h_ref, sem):
+    spans = [pl.ds(start, PIECE) for start in range(0, NZ * NY * RD, PIECE)]
+    pieces = [pltpu.make_async_copy(h_hbm.at[:, span], h_ref.at[:, span], sem.at[i]) for i, span in enumerate(spans)]
+    for piece in pieces:
+        piece.start()
     total = jnp.sum(p_ref[...].astype(F32), axis=0)
-    half_ref[...] = total[:, :W].astype(BF16)
     diag_ref[:, 0:128] = total[0:2, W:]
     diag_ref[:, 128:] = total[2:4, W:]
+    half = total[:, :W].astype(BF16)
+    for piece, span in zip(pieces, spans, strict=True):
+        piece.wait()
+        energy_ref[:, span] = jnp.dot(half, h_ref[:, span], preferred_element_type=F32).astype(BF16)
 
 
 def per_device(trailing, panel, diag_inverse, pole_weights, owner_map, ham_slab):
@@ -199,9 +211,16 @@
         join_kernel, [((NX * NY, CAP, W + 128), BF16)], [SM, VM, VM, VM, VM], moved=1 << 18
     )(pole_weights, quad, diag_inverse, mine, other)
     joined = lax.all_to_all(joined, ("x", "y"), 0, 0)
-    half, diag = kernel_call(total_kernel, [((CAP, W), BF16), ((2, W), F32)], [VM], moved=1 << 18)(joined)
-    density_diag = diag + lax.ppermute(diag, "c", swap)
-    patch_energy = jnp.dot(half, ham_slab, preferred_element_type=F32).astype(BF16)
+    diag, patch_energy = kernel_call(
+        total_kernel,
+        [((2, W), F32), ((CAP, NZ * NY * RD), BF16)],
+        [VM, pl.BlockSpec(memory_space=pl.ANY)],
+        flops=1 << 24,
+        moved=1 << 21,
+        kept=(True, False),
+        scratch=[pltpu.VMEM((W, NZ * NY * RD), BF16), pltpu.SemaphoreType.DMA((NZ * NY * RD // PIECE,))],
+    )(joined, ham_slab)
+    density_diag = lax.psum(diag, "c")
     return (density_diag, patch_energy)
 
 

time: 103 us -> 103 us (level)
  blocking collectives: 56.6 us -> 69 us
  starting transfers between devices: 31.8 us -> 20.3 us
  matrix products: 2.61 us -> 0 us
  Pallas kernels: 5.58 us -> 7.86 us
    psum x0 -> x1, blocking collectives: none -> 12.4 us  [per_device(): density_diag = lax.psum(diag, 'c')]
    ppermute x1 -> x0, starting transfers between devices: 11.6 us -> none  [per_device(): density_diag = diag + lax.ppermute(diag, 'c', swap)]
    dot_general x1 -> x0, matrix products: 2.61 us -> none  [per_device(): jnp.dot(half, ham_slab, preferred_element_type=F32).astype(BF16)]
    pallas_call x4, Pallas kernels: 3.06 us -> 5.47 us  [run(): call(*(pltpu.with_memory_space_constraint(arg, pltpu.VMEM) if spec is VM...]
  transfers between devices with their start and end apart: 4 -> 3, of which waited for: 2 -> 2; matrix products, arithmetic and copies ran while one was open for 3% -> 0% of each run, Pallas kernels for 0% -> 0%
where the time goes in v5:
time: 103 us
  blocking collectives  69 us (67%)
  starting transfers between devices  20.3 us (20%)
  Pallas kernels  7.86 us (8%)
  waiting for transfers between devices  4.69 us (5%)
    all_gather x1, blocking collectives, per_device(): columns = lax.all_gather(own, 'z')  39.4 us
    all_to_all x1, blocking collectives, per_device(): joined = lax.all_to_all(joined, ('x', 'y'), 0, 0)  17.3 us
    psum x1, blocking collectives, per_device(): density_diag = lax.psum(diag, 'c')  12.4 us
    all_to_all x1, starting transfers between devices, per_device(): block = lax.all_to_all(packed, 'y', 0, 0)  7.65 us
    ppermute x1, starting transfers between devices, per_device(): other = lax.ppermute(other, 'c', swap)  7.03 us
    all_to_all x1, starting transfers between devices, per_device(): quad = lax.all_to_all(quad, 'z', 0, 0)  5.59 us
    pallas_call x4, Pallas kernels, run(): call(*(pltpu.with_memory_space_constraint(arg, pltpu.VMEM) if spec is VM...  5.47 us
    all_to_all x1, waiting for transfers between devices, per_device(): quad = lax.all_to_all(quad, 'z', 0, 0)  3.72 us
  transfers between devices with their start and end apart: 3, of which 2 were waited for; matrix products, arithmetic and copies ran while one was open for 0% of the time, Pallas kernels for 0%

profile of v5, /device:TPU:1, one launch (start us, length us, event | category | flops | bytes accessed | tf_op | source)
XLA Modules:
  0.0 102.5 jit_solution(3168922858998839501)
XLA Ops:
  0.6 2.4 %pack.1 = (bf16[8,112,512]{2,1,0:T(8,128)(2,1)}, bf16[32,512]{1,0:T(8,128)(2,1)S(1)}) custom-call(s32[1,32]{1,0:T(1,128)} %bitcast.3, bf16[1,2,32,4096]{3,2,1,0:T(8,128)(2,1)} %g_hbm.1, bf16[1,2,32,256]{3,2,1,0:T(8,128)(2,1)} %l_hbm.1), custom_call_target="tpu_custom_call" | custom-call | bytes 1048576 | tf_op jit(solution)/shard_map/pack/pallas_call | solution.py:117
  3.0 0.0 copy-start
  3.0 7.7 %all-to-all-start = ((bf16[8,112,512]{2,1,0:T(8,128)(2,1)}), bf16[8,112,512]{2,1,0:T(8,128)(2,1)S(1)}, u32[]{:S(2)}, u32[]{:S(2)}) async-start(bf16[8,112,512]{2,1,0:T(8,128)(2,1)} %get-tuple-element.10), calls=%async_computation | async-start | bytes 1835008 | tf_op jit(solution)/shard_map/all_to_all | solution.py:199
  10.7 39.4 %all-gather = bf16[512,512]{1,0:T(8,128)(2,1)S(1)} all-gather(bf16[32,512]{1,0:T(8,128)(2,1)S(1)} %get-tuple-element.11), channel_id=2, replica_groups=mesh['x'=4,'c'=2,'z'=16,'y'=8] {'z'}, dimensions={0}, use_global_device_ids=true | all-gather | bytes 557056 | tf_op jit(solution)/shard_map/all_gather | solution.py:200
  50.1 0.0 all-to-all-done.b_ref
  50.1 2.1 %shard_map.77 = (bf16[256,256]{1,0:T(8,128)(2,1)S(1)}, bf16[16,16,256]{2,1,0:T(8,128)(2,1)}) custom-call(f32[1,2]{1,0:T(1,128)} %w_ref.3, bf16[8,112,512]{2,1,0:T(8,128)(2,1)S(1)} %all-to-all-done.b_ref, bf16[16,32,512]{2,1,0:T(8,128)(2,1)S(1)} %bitcast.2), custom_call_target="tpu_custom_call" | custom-call | flops 536870912 | bytes 1048576 | tf_op jit(solution)/shard_map/pallas_call | solution.py:33
  52.2 5.6 %all-to-all-start.1 = ((bf16[16,16,256]{2,1,0:T(8,128)(2,1)}), bf16[16,16,256]{2,1,0:T(8,128)(2,1)S(1)}, u32[]{:S(2)}, u32[]{:S(2)}) async-start(bf16[16,16,256]{2,1,0:T(8,128)(2,1)} %get-tuple-element.12), calls=%async_computation.1 | async-start | bytes 262144 | tf_op jit(solution)/shard_map/all_to_all | solution.py:204
  57.8 0.2 shard_map.78
  58.0 7.0 %collective-permute-start = (bf16[32,8,256]{2,1,0:T(8,128)(2,1)S(1)}, bf16[32,8,256]{2,1,0:T(8,128)(2,1)S(1)}, u32[]{:S(2)}, u32[]{:S(2)}) collective-permute-start(bf16[32,8,256]{2,1,0:T(8,128)(2,1)S(1)} %get-tuple-element.15), channel_id=1, source_target_pairs={{0,128},{128,0},{1,129},{129,1},{2,130},{130,2},{3,131},{131,3},{4... | collective-permute-start | bytes 393224 | tf_op jit(solution)/shard_map/ppermute | solution.py:209
  65.0 1.0 collective-permute-done.o_ref
  66.0 3.7 %all-to-all-done.1.q_ref = bf16[16,16,256]{2,1,0:T(8,128)(2,1)S(1)} async-done(((bf16[16,16,256]{2,1,0:T(8,128)(2,1)}), bf16[16,16,256]{2,1,0:T(8,128)(2,1)S(1)}, u32[]{:S(2)}, u32[]{:S(2)}) %all-to-all-start.1) | async-done | bytes 131104 | tf_op jit(solution)/shard_map/all_to_all | solution.py:204
  69.7 0.0 copy-done
  69.7 0.7 shard_map.79
  70.5 17.3 %all_to_all.15.p_ref = bf16[32,8,384]{2,1,0:T(8,128)(2,1)S(1)} all-to-all(bf16[32,8,384]{2,1,0:T(8,128)(2,1)S(1)} %shard_map.79), channel_id=1, replica_groups=mesh['x'=4,'c'=2,'z'=16,'y'=8] {'x','y'}, dimensions={0} | all-to-all | bytes 393216 | tf_op jit(solution)/shard_map/all_to_all | solution.py:213
  87.7 2.4 %shard_map.80 = (f32[2,256]{1,0:T(2,128)S(1)}, bf16[8,4096]{1,0:T(8,128)(2,1)}) custom-call(bf16[32,8,384]{2,1,0:T(8,128)(2,1)S(1)} %all_to_all.15.p_ref, bf16[256,4096]{1,0:T(8,128)(2,1)} %h_hbm.1), custom_call_target="tpu_custom_call" | custom-call | flops 16777216 | bytes 2097152 | tf_op jit(solution)/shard_map/pallas_call | solution.py:33
  90.2 12.4 %psum.7 = f32[2,256]{1,0:T(2,128)} all-reduce(f32[2,256]{1,0:T(2,128)S(1)} %get-tuple-element.16), channel_id=1, replica_groups=mesh['x'=4,'c'=2,'z'=16,'y'=8] {'c'}, use_global_device_ids=true, to_apply=%region_0.0 | all-reduce | flops 512 | bytes 4096 | tf_op jit(solution)/shard_map/psum | solution.py:223
  (1 shorter events, 0.0 us)
Async XLA Ops:
  3.0 66.7 %copy-start = (bf16[1,2,2,256]{3,2,1,0:T(2,128)(2,1)S(1)}, bf16[1,2,2,256]{3,2,1,0:T(2,128)(2,1)}, u32[]{:S(2)}) copy-start(bf16[1,2,2,256]{3,2,1,0:T(2,128)(2,1)} %d_ref.1) | copy-start | bytes 6148
  3.0 47.0 %all-to-all-start = ((bf16[8,112,512]{2,1,0:T(8,128)(2,1)}), bf16[8,112,512]{2,1,0:T(8,128)(2,1)S(1)}, u32[]{:S(2)}, u32[]{:S(2)}) async-start(bf16[8,112,512]{2,1,0:T(8,128)(2,1)} %get-tuple-element.10), calls=%async_computation | async-start | bytes 1835008 | tf_op jit(solution)/shard_map/all_to_all | solution.py:199
  52.2 17.6 %all-to-all-start.1 = ((bf16[16,16,256]{2,1,0:T(8,128)(2,1)}), bf16[16,16,256]{2,1,0:T(8,128)(2,1)S(1)}, u32[]{:S(2)}, u32[]{:S(2)}) async-start(bf16[16,16,256]{2,1,0:T(8,128)(2,1)} %get-tuple-element.12), calls=%async_computation.1 | async-start | bytes 262144 | tf_op jit(solution)/shard_map/all_to_all | solution.py:204
  58.0 8.0 %collective-permute-start = (bf16[32,8,256]{2,1,0:T(8,128)(2,1)S(1)}, bf16[32,8,256]{2,1,0:T(8,128)(2,1)S(1)}, u32[]{:S(2)}, u32[]{:S(2)}) collective-permute-start(bf16[32,8,256]{2,1,0:T(8,128)(2,1)S(1)} %get-tuple-element.15), channel_id=1, source_target_pairs={{0,128},{128,0},{1,129},{129,1},{2,130},{130,2},{3,131},{131,3},{4... | collective-permute-start | bytes 393224 | tf_op jit(solution)/shard_map/ppermute | solution.py:209

commit v6 on v5

--- a/solution.py
+++ b/solution.py
@@ -12,6 +12,8 @@
 YC = NZ * RD
 CAP = 8
 TAIL = 16
+HOLD = 1
+HELD = 3072
 PIECE = 1024
 F32 = jnp.float32
 BF16 = jnp.bfloat16
@@ -19,7 +21,7 @@
 SM = pl.BlockSpec(memory_space=pltpu.SMEM)
 
 
-def kernel_call(body, outs, specs, flops=0, moved=0, kept=(True, True), scratch=()):
+def kernel_call(body, outs, specs, flops=0, moved=0, kept=(True,) * 8, scratch=()):
     call = pl.pallas_call(
         body,
         out_shape=tuple(pltpu.VMEM(s, d) if k else jax.ShapeDtypeStruct(s, d) for (s, d), k in zip(outs, kept)),
@@ -150,29 +152,32 @@
     density_ref[...] = (-even).astype(BF16)
 
 
-def place_kernel(s_ref, density_ref, mine_ref, other_ref):
-    core = lax.axis_index("c")
-    line = lax.broadcasted_iota(jnp.int32, (2 * NX * CAP, RD), 0)
-    half = line // (NX * CAP)
-    within = line % (NX * CAP)
-    side = jnp.where(half == 0, core, 1 - core)
-    index = (within // CAP * NC + side) * CAP + within % CAP
+def place_kernel(s_ref, d_ref, o_ref, h_hbm, out_ref, *rest):
+    slabs, sem = rest[:-1], rest[-1]
+    pieces = [
+        pltpu.make_async_copy(h_hbm.at[:, pl.ds(HELD * i, HELD)], slab, sem.at[i]) for i, slab in enumerate(slabs)
+    ]
+    for piece in pieces:
+        piece.start()
+    line = lax.broadcasted_iota(jnp.int32, (NX * CAP, RD), 0)
+    index = (line // CAP * NC + lax.axis_index("c")) * CAP + line % CAP
+    rows = (d_ref[...].astype(F32) + o_ref[...].astype(F32)).astype(BF16)
     for y in range(NY):
         slot = s_ref[y, 0:1, 0:RD].astype(F32).astype(jnp.int32)
         place = (index == slot).astype(F32).astype(BF16)
-        rows = density_ref[RD * y : RD * y + RD, :]
-        placed = jnp.dot(place, rows, preferred_element_type=F32).astype(BF16)
+        placed = jnp.dot(place, rows[RD * y : RD * y + RD], preferred_element_type=F32).astype(BF16)
         for x in range(NX):
-            mine_ref[NY * x + y] = placed[CAP * x : CAP * x + CAP]
-            other_ref[NY * x + y] = placed[CAP * (NX + x) : CAP * (NX + x) + CAP]
-
-
-def join_kernel(w_ref, q_ref, d_ref, p_ref, o_ref, out_ref):
+            out_ref[NY * x + y] = placed[CAP * x : CAP * x + CAP]
+    for piece in pieces:
+        piece.wait()
+
+
+def join_kernel(w_ref, q_ref, d_ref, p_ref, out_ref):
     quad = jnp.sum(q_ref[...].astype(F32), axis=0)
     diag = w_ref[0, 0] * d_ref[0, 1].astype(F32) + w_ref[0, 1] * d_ref[0, 0].astype(F32)
     here = lax.axis_index("y")
     zero = jnp.zeros((CAP - 4, 128), F32)
-    out_ref[:, :, 0:W] = (p_ref[...].astype(F32) + o_ref[...].astype(F32)).astype(BF16)
+    out_ref[:, :, 0:W] = p_ref[...]
     for y in range(NY):
         rows = quad[2 * y : 2 * y + 2] + jnp.where(here == y, diag, 0.0)
         tail = jnp.concatenate([rows[:, :128], rows[:, 128:], zero], axis=0).astype(BF16)
@@ -180,18 +185,27 @@
             out_ref[NY * x + y, :, W:] = tail
 
 
-def total_kernel(p_ref, h_hbm, diag_ref, energy_ref, h_ref, sem):
-    spans = [pl.ds(start, PIECE) for start in range(0, NZ * NY * RD, PIECE)]
-    pieces = [pltpu.make_async_copy(h_hbm.at[:, span], h_ref.at[:, span], sem.at[i]) for i, span in enumerate(spans)]
+def total_kernel(p_ref, *refs):
+    slabs, (h_hbm, diag_ref, energy_ref, h_ref, sem) = refs[:HOLD], refs[HOLD:]
+    held = HOLD * HELD
+    spans = [pl.ds(start, PIECE) for start in range(0, NZ * NY * RD - held, PIECE)]
+    pieces = [
+        pltpu.make_async_copy(h_hbm.at[:, pl.ds(held + PIECE * i, PIECE)], h_ref.at[:, span], sem.at[i])
+        for i, span in enumerate(spans)
+    ]
     for piece in pieces:
         piece.start()
     total = jnp.sum(p_ref[...].astype(F32), axis=0)
     diag_ref[:, 0:128] = total[0:2, W:]
     diag_ref[:, 128:] = total[2:4, W:]
     half = total[:, :W].astype(BF16)
-    for piece, span in zip(pieces, spans, strict=True):
+    for i, slab in enumerate(slabs):
+        span = pl.ds(HELD * i, HELD)
+        energy_ref[:, span] = jnp.dot(half, slab[...], preferred_element_type=F32).astype(BF16)
+    for i, (piece, span) in enumerate(zip(pieces, spans, strict=True)):
         piece.wait()
-        energy_ref[:, span] = jnp.dot(half, h_ref[:, span], preferred_element_type=F32).astype(BF16)
+        to = pl.ds(held + PIECE * i, PIECE)
+        energy_ref[:, to] = jnp.dot(half, h_ref[:, span], preferred_element_type=F32).astype(BF16)
 
 
 def per_device(trailing, panel, diag_inverse, pole_weights, owner_map, ham_slab):
@@ -202,24 +216,29 @@
         cross_kernel, [((ZR, W), BF16), ((NZ, W // NZ, W), BF16)], [SM, VM, VM], flops=1 << 29, moved=1 << 20
     )(pole_weights, block, columns)
     quad = lax.all_to_all(quad, "z", 0, 0)
-    mine, other = kernel_call(
-        place_kernel, [((NX * NY, CAP, W), BF16)] * 2, [VM, VM], flops=1 << 23, moved=1 << 18
-    )(block[:, 3 * RD :, :128], density)
-    swap = ((0, 1), (1, 0))
-    other = lax.ppermute(other, "c", swap)
+    other = lax.ppermute(density, "c", ((0, 1), (1, 0)))
+    placed, *slabs = kernel_call(
+        place_kernel,
+        [((NX * NY, CAP, W), BF16)] + [((W, HELD), BF16)] * HOLD,
+        [VM, VM, VM, pl.BlockSpec(memory_space=pl.ANY)],
+        flops=1 << 23,
+        moved=1 << 21,
+        scratch=[pltpu.SemaphoreType.DMA((HOLD,))],
+    )(block[:, 3 * RD :, :128], density, other, ham_slab)
     (joined,) = kernel_call(
-        join_kernel, [((NX * NY, CAP, W + 128), BF16)], [SM, VM, VM, VM, VM], moved=1 << 18
-    )(pole_weights, quad, diag_inverse, mine, other)
+        join_kernel, [((NX * NY, CAP, W + 128), BF16)], [SM, VM, VM, VM], moved=1 << 18
+    )(pole_weights, quad, diag_inverse, placed)
     joined = lax.all_to_all(joined, ("x", "y"), 0, 0)
+    streamed = NZ * NY * RD - HOLD * HELD
     diag, patch_energy = kernel_call(
         total_kernel,
         [((2, W), F32), ((CAP, NZ * NY * RD), BF16)],
-        [VM, pl.BlockSpec(memory_space=pl.ANY)],
+        [VM] * (1 + HOLD) + [pl.BlockSpec(memory_space=pl.ANY)],
         flops=1 << 24,
-        moved=1 << 21,
+        moved=1 << 18,
         kept=(True, False),
-        scratch=[pltpu.VMEM((W, NZ * NY * RD), BF16), pltpu.SemaphoreType.DMA((NZ * NY * RD // PIECE,))],
-    )(joined, ham_slab)
+        scratch=[pltpu.VMEM((W, streamed), BF16), pltpu.SemaphoreType.DMA((streamed // PIECE,))],
+    )(joined, *slabs, ham_slab)
     density_diag = lax.psum(diag, "c")
     return (density_diag, patch_energy)
 

time: 103 us -> 103 us (level)
  waiting for transfers between devices: 4.69 us -> 3.48 us
    all_to_all x1, waiting for transfers between devices: 3.72 us -> 2.52 us  [per_device(): quad = lax.all_to_all(quad, 'z', 0, 0)]
  transfers between devices with their start and end apart: 3 -> 3, of which waited for: 2 -> 2; matrix products, arithmetic and copies ran while one was open for 0% -> 0% of each run, Pallas kernels for 0% -> 1%
where the time goes in v6:
time: 103 us; the launch traced here: 102 us
  blocking collectives  69 us (67%)
  starting transfers between devices  20.3 us (20%)
  Pallas kernels  8.82 us (9%)
  waiting for transfers between devices  3.48 us (3%)
    all_gather x1, blocking collectives, per_device(): columns = lax.all_gather(own, 'z')  39.4 us
    all_to_all x1, blocking collectives, per_device(): joined = lax.all_to_all(joined, ('x', 'y'), 0, 0)  17.3 us
    psum x1, blocking collectives, per_device(): density_diag = lax.psum(diag, 'c')  12.4 us
    all_to_all x1, starting transfers between devices, per_device(): block = lax.all_to_all(packed, 'y', 0, 0)  7.65 us
    ppermute x1, starting transfers between devices, per_device(): other = lax.ppermute(density, 'c', ((0, 1), (1, 0)))  7.02 us
    pallas_call x4, Pallas kernels, run(): call(*(pltpu.with_memory_space_constraint(arg, pltpu.VMEM) if spec is VM...  6.43 us
    all_to_all x1, starting transfers between devices, per_device(): quad = lax.all_to_all(quad, 'z', 0, 0)  5.59 us
    all_to_all x1, waiting for transfers between devices, per_device(): quad = lax.all_to_all(quad, 'z', 0, 0)  2.52 us
  transfers between devices with their start and end apart: 3, of which 2 were waited for; matrix products, arithmetic and copies ran while one was open for 0% of the time, Pallas kernels for 1%

profile of v6, /device:TPU:1, one launch (start us, length us, event | category | flops | bytes accessed | tf_op | source)
XLA Modules:
  0.0 102.3 jit_solution(8427332548276179697)
XLA Ops:
  0.6 2.4 %pack.1 = (bf16[8,112,512]{2,1,0:T(8,128)(2,1)}, bf16[32,512]{1,0:T(8,128)(2,1)S(1)}) custom-call(s32[1,32]{1,0:T(1,128)} %bitcast.3, bf16[1,2,32,4096]{3,2,1,0:T(8,128)(2,1)} %g_hbm.1, bf16[1,2,32,256]{3,2,1,0:T(8,128)(2,1)} %l_hbm.1), custom_call_target="tpu_custom_call" | custom-call | bytes 1048576 | tf_op jit(solution)/shard_map/pack/pallas_call | solution.py:119
  3.0 7.7 %all-to-all-start = ((bf16[8,112,512]{2,1,0:T(8,128)(2,1)}), bf16[8,112,512]{2,1,0:T(8,128)(2,1)S(1)}, u32[]{:S(2)}, u32[]{:S(2)}) async-start(bf16[8,112,512]{2,1,0:T(8,128)(2,1)} %get-tuple-element.10), calls=%async_computation | async-start | bytes 1835008 | tf_op jit(solution)/shard_map/all_to_all | solution.py:213
  10.7 39.4 %all-gather = bf16[512,512]{1,0:T(8,128)(2,1)S(1)} all-gather(bf16[32,512]{1,0:T(8,128)(2,1)S(1)} %get-tuple-element.11), channel_id=2, replica_groups=mesh['x'=4,'c'=2,'z'=16,'y'=8] {'z'}, dimensions={0}, use_global_device_ids=true | all-gather | bytes 557056 | tf_op jit(solution)/shard_map/all_gather | solution.py:214
  50.1 0.0 all-to-all-done.b_ref
  50.1 0.0 copy-start
  50.1 2.2 %shard_map.77 = (bf16[256,256]{1,0:T(8,128)(2,1)S(1)}, bf16[16,16,256]{2,1,0:T(8,128)(2,1)}) custom-call(f32[1,2]{1,0:T(1,128)} %w_ref.3, bf16[8,112,512]{2,1,0:T(8,128)(2,1)S(1)} %all-to-all-done.b_ref, bf16[16,32,512]{2,1,0:T(8,128)(2,1)S(1)} %bitcast.2), custom_call_target="tpu_custom_call" | custom-call | flops 536870912 | bytes 1048576 | tf_op jit(solution)/shard_map/pallas_call | solution.py:35
  52.3 5.6 %all-to-all-start.1 = ((bf16[16,16,256]{2,1,0:T(8,128)(2,1)}), bf16[16,16,256]{2,1,0:T(8,128)(2,1)S(1)}, u32[]{:S(2)}, u32[]{:S(2)}) async-start(bf16[16,16,256]{2,1,0:T(8,128)(2,1)} %get-tuple-element.12), calls=%async_computation.1 | async-start | bytes 262144 | tf_op jit(solution)/shard_map/all_to_all | solution.py:218
  57.9 7.0 %collective-permute-start = (bf16[256,256]{1,0:T(8,128)(2,1)S(1)}, bf16[256,256]{1,0:T(8,128)(2,1)S(1)}, u32[]{:S(2)}, u32[]{:S(2)}) collective-permute-start(bf16[256,256]{1,0:T(8,128)(2,1)S(1)} %get-tuple-element.13.d_ref), channel_id=1, source_target_pairs={{0,128},{128,0},{1,129},{129,1},{2,130},{130,2},{3,131},{131,3},{4... | collective-permute-start | bytes 393224 | tf_op jit(solution)/shard_map/ppermute | solution.py:219
  64.9 0.9 collective-permute-done.o_ref
  65.9 1.4 %shard_map.78 = (bf16[32,8,256]{2,1,0:T(8,128)(2,1)S(1)}, bf16[256,3072]{1,0:T(8,128)(2,1)S(1)}) custom-call(bf16[8,16,128]{2,1,0:T(8,128)(2,1)S(1)} %slice.4.s_ref, bf16[256,256]{1,0:T(8,128)(2,1)S(1)} %get-tuple-element.13.d_ref, bf16[256,256]{1,0:T(8,128)(2,1)S(1)} %collective-permute-done.o_ref, bf16[256,4096]{1,0:T(8,128)(2,1)} %refs_1_.1), custom_call_target="tpu_custom_call" | custom-call | flops 8388608 | bytes 2097152 | tf_op jit(solution)/shard_map/pallas_call | solution.py:35
  67.3 2.5 %all-to-all-done.1.q_ref = bf16[16,16,256]{2,1,0:T(8,128)(2,1)S(1)} async-done(((bf16[16,16,256]{2,1,0:T(8,128)(2,1)}), bf16[16,16,256]{2,1,0:T(8,128)(2,1)S(1)}, u32[]{:S(2)}, u32[]{:S(2)}) %all-to-all-start.1) | async-done | bytes 131104 | tf_op jit(solution)/shard_map/all_to_all | solution.py:218
  69.8 0.0 copy-done
  69.8 0.7 shard_map.79
  70.6 17.3 %all_to_all.15.p_ref = bf16[32,8,384]{2,1,0:T(8,128)(2,1)S(1)} all-to-all(bf16[32,8,384]{2,1,0:T(8,128)(2,1)S(1)} %shard_map.79), channel_id=1, replica_groups=mesh['x'=4,'c'=2,'z'=16,'y'=8] {'x','y'}, dimensions={0} | all-to-all | bytes 393216 | tf_op jit(solution)/shard_map/all_to_all | solution.py:231
  87.8 2.1 %shard_map.80 = (f32[2,256]{1,0:T(2,128)S(1)}, bf16[8,4096]{1,0:T(8,128)(2,1)}) custom-call(bf16[32,8,384]{2,1,0:T(8,128)(2,1)S(1)} %all_to_all.15.p_ref, bf16[256,3072]{1,0:T(8,128)(2,1)S(1)} %get-tuple-element.15.refs_0_, bf16[256,4096]{1,0:T(8,128)(2,1)} %refs_1_.1), custom_call_target="tpu_custom_call" | custom-call | flops 16777216 | bytes 262144 | tf_op jit(solution)/shard_map/pallas_call | solution.py:35
  89.9 12.4 %psum.7 = f32[2,256]{1,0:T(2,128)} all-reduce(f32[2,256]{1,0:T(2,128)S(1)} %get-tuple-element.16), channel_id=1, replica_groups=mesh['x'=4,'c'=2,'z'=16,'y'=8] {'c'}, use_global_device_ids=true, to_apply=%region_0.0 | all-reduce | flops 512 | bytes 4096 | tf_op jit(solution)/shard_map/psum | solution.py:242
  (1 shorter events, 0.0 us)
Async XLA Ops:
  3.0 47.0 %all-to-all-start = ((bf16[8,112,512]{2,1,0:T(8,128)(2,1)}), bf16[8,112,512]{2,1,0:T(8,128)(2,1)S(1)}, u32[]{:S(2)}, u32[]{:S(2)}) async-start(bf16[8,112,512]{2,1,0:T(8,128)(2,1)} %get-tuple-element.10), calls=%async_computation | async-start | bytes 1835008 | tf_op jit(solution)/shard_map/all_to_all | solution.py:213
  50.1 19.8 %copy-start = (bf16[1,2,2,256]{3,2,1,0:T(2,128)(2,1)S(1)}, bf16[1,2,2,256]{3,2,1,0:T(2,128)(2,1)}, u32[]{:S(2)}) copy-start(bf16[1,2,2,256]{3,2,1,0:T(2,128)(2,1)} %d_ref.1) | copy-start | bytes 6148
  52.3 17.6 %all-to-all-start.1 = ((bf16[16,16,256]{2,1,0:T(8,128)(2,1)}), bf16[16,16,256]{2,1,0:T(8,128)(2,1)S(1)}, u32[]{:S(2)}, u32[]{:S(2)}) async-start(bf16[16,16,256]{2,1,0:T(8,128)(2,1)} %get-tuple-element.12), calls=%async_computation.1 | async-start | bytes 262144 | tf_op jit(solution)/shard_map/all_to_all | solution.py:218
  57.9 8.0 %collective-permute-start = (bf16[256,256]{1,0:T(8,128)(2,1)S(1)}, bf16[256,256]{1,0:T(8,128)(2,1)S(1)}, u32[]{:S(2)}, u32[]{:S(2)}) collective-permute-start(bf16[256,256]{1,0:T(8,128)(2,1)S(1)} %get-tuple-element.13.d_ref), channel_id=1, source_target_pairs={{0,128},{128,0},{1,129},{129,1},{2,130},{130,2},{3,131},{131,3},{4... | collective-permute-start | bytes 393224 | tf_op jit(solution)/shard_map/ppermute | solution.py:219

commit v7 on v6

--- a/solution.py
+++ b/solution.py
@@ -134,7 +134,7 @@
     )(owner_map.reshape(1, RD), trailing, panel)
 
 
-def cross_kernel(w_ref, b_ref, l_ref, density_ref, quad_ref):
+def cross_kernel(w_ref, b_ref, l_ref, d_ref, out_ref):
     wr = w_ref[0, 0]
     wi = w_ref[0, 1]
     columns = l_ref[...].reshape(YC, 2 * W)
@@ -148,11 +148,21 @@
     over_rows = (((0,), (0,)), ((), ()))
     quad = lax.dot_general(rows[:, :W], even.astype(BF16), over_rows, preferred_element_type=F32)
     quad = quad + lax.dot_general(rows[:, W:], odd.astype(BF16), over_rows, preferred_element_type=F32)
-    quad_ref[...] = quad.astype(BF16).reshape(NZ, W // NZ, W)
-    density_ref[...] = (-even).astype(BF16)
-
-
-def place_kernel(s_ref, d_ref, o_ref, h_hbm, out_ref, *rest):
+    diag = wr * d_ref[0, 1].astype(F32) + wi * d_ref[0, 0].astype(F32)
+    at = lax.axis_index("z") * (2 * NY) + lax.axis_index("y") * 2
+    line = lax.broadcasted_iota(jnp.int32, (W, W), 0)
+    for row in range(2):
+        quad = quad + jnp.where(line == at + row, diag[row : row + 1], 0.0)
+    out_ref[:, 0:W] = (-even).astype(BF16)
+    out_ref[:, W:] = quad.astype(BF16)
+
+
+def pair_kernel(p_ref, density_ref, quad_ref):
+    quad_ref[...] = (p_ref[0, :, W:].astype(F32) + p_ref[1, :, W:].astype(F32)).astype(BF16).reshape(NZ, W // NZ, W)
+    density_ref[...] = (p_ref[0, :, 0:W].astype(F32) + p_ref[1, :, 0:W].astype(F32)).astype(BF16)
+
+
+def place_kernel(s_ref, d_ref, h_hbm, out_ref, *rest):
     slabs, sem = rest[:-1], rest[-1]
     pieces = [
         pltpu.make_async_copy(h_hbm.at[:, pl.ds(HELD * i, HELD)], slab, sem.at[i]) for i, slab in enumerate(slabs)
@@ -161,7 +171,7 @@
         piece.start()
     line = lax.broadcasted_iota(jnp.int32, (NX * CAP, RD), 0)
     index = (line // CAP * NC + lax.axis_index("c")) * CAP + line % CAP
-    rows = (d_ref[...].astype(F32) + o_ref[...].astype(F32)).astype(BF16)
+    rows = d_ref[...]
     for y in range(NY):
         slot = s_ref[y, 0:1, 0:RD].astype(F32).astype(jnp.int32)
         place = (index == slot).astype(F32).astype(BF16)
@@ -172,14 +182,12 @@
         piece.wait()
 
 
-def join_kernel(w_ref, q_ref, d_ref, p_ref, out_ref):
+def join_kernel(q_ref, p_ref, out_ref):
     quad = jnp.sum(q_ref[...].astype(F32), axis=0)
-    diag = w_ref[0, 0] * d_ref[0, 1].astype(F32) + w_ref[0, 1] * d_ref[0, 0].astype(F32)
-    here = lax.axis_index("y")
     zero = jnp.zeros((CAP - 4, 128), F32)
     out_ref[:, :, 0:W] = p_ref[...]
     for y in range(NY):
-        rows = quad[2 * y : 2 * y + 2] + jnp.where(here == y, diag, 0.0)
+        rows = quad[2 * y : 2 * y + 2]
         tail = jnp.concatenate([rows[:, :128], rows[:, 128:], zero], axis=0).astype(BF16)
         for x in range(NX):
             out_ref[NY * x + y, :, W:] = tail
@@ -212,34 +220,32 @@
     packed, own = pack(owner_map, trailing, panel)
     block = lax.all_to_all(packed, "y", 0, 0)
     columns = lax.all_gather(own, "z")
-    density, quad = kernel_call(
-        cross_kernel, [((ZR, W), BF16), ((NZ, W // NZ, W), BF16)], [SM, VM, VM], flops=1 << 29, moved=1 << 20
-    )(pole_weights, block, columns)
+    (partial,) = kernel_call(
+        cross_kernel, [((ZR, 2 * W), BF16)], [SM, VM, VM, VM], flops=1 << 29, moved=1 << 20
+    )(pole_weights, block, columns, diag_inverse)
+    both = lax.all_gather(partial, "c")
+    density, quad = kernel_call(pair_kernel, [((ZR, W), BF16), ((NZ, W // NZ, W), BF16)], [VM], moved=1 << 19)(both)
     quad = lax.all_to_all(quad, "z", 0, 0)
-    other = lax.ppermute(density, "c", ((0, 1), (1, 0)))
     placed, *slabs = kernel_call(
         place_kernel,
         [((NX * NY, CAP, W), BF16)] + [((W, HELD), BF16)] * HOLD,
-        [VM, VM, VM, pl.BlockSpec(memory_space=pl.ANY)],
+        [VM, VM, pl.BlockSpec(memory_space=pl.ANY)],
         flops=1 << 23,
         moved=1 << 21,
         scratch=[pltpu.SemaphoreType.DMA((HOLD,))],
-    )(block[:, 3 * RD :, :128], density, other, ham_slab)
-    (joined,) = kernel_call(
-        join_kernel, [((NX * NY, CAP, W + 128), BF16)], [SM, VM, VM, VM], moved=1 << 18
-    )(pole_weights, quad, diag_inverse, placed)
+    )(block[:, 3 * RD :, :128], density, ham_slab)
+    (joined,) = kernel_call(join_kernel, [((NX * NY, CAP, W + 128), BF16)], [VM, VM], moved=1 << 18)(quad, placed)
     joined = lax.all_to_all(joined, ("x", "y"), 0, 0)
     streamed = NZ * NY * RD - HOLD * HELD
-    diag, patch_energy = kernel_call(
+    density_diag, patch_energy = kernel_call(
         total_kernel,
         [((2, W), F32), ((CAP, NZ * NY * RD), BF16)],
         [VM] * (1 + HOLD) + [pl.BlockSpec(memory_space=pl.ANY)],
         flops=1 << 24,
         moved=1 << 18,
-        kept=(True, False),
+        kept=(False, False),
         scratch=[pltpu.VMEM((W, streamed), BF16), pltpu.SemaphoreType.DMA((streamed // PIECE,))],
     )(joined, *slabs, ham_slab)
-    density_diag = lax.psum(diag, "c")
     return (density_diag, patch_energy)
 
 

time: 103 us -> 102 us (level)
  the two profiles are of different devices: /device:TPU:1 before, /device:TPU:8 now
where the time goes in v7:
time: 102 us; the launch traced here: 101 us
  blocking collectives  58.6 us (57%)
  starting transfers between devices  20.6 us (20%)
  waiting for transfers between devices  13.3 us (13%)
  Pallas kernels  8.05 us (8%)
    all_gather x1, blocking collectives, per_device(): columns = lax.all_gather(own, 'z')  36.3 us
    all_to_all x1, blocking collectives, per_device(): joined = lax.all_to_all(joined, ('x', 'y'), 0, 0)  20.1 us
    all_to_all x1, starting transfers between devices, per_device(): block = lax.all_to_all(packed, 'y', 0, 0)  16.5 us
    all_to_all x1, waiting for transfers between devices, per_device(): quad = lax.all_to_all(quad, 'z', 0, 0)  13.3 us
    pallas_call x5, Pallas kernels, run(): call(*(pltpu.with_memory_space_constraint(arg, pltpu.VMEM) if spec is VM...  5.65 us
    all_to_all x1, starting transfers between devices, per_device(): quad = lax.all_to_all(quad, 'z', 0, 0)  4.04 us
    pallas_call x1, Pallas kernels, pack(): pl.pallas_call(pack_kernel, out_shape=(jax.ShapeDtypeStruct(packed, BF16)...  2.4 us
    all_gather x1, blocking collectives, per_device(): both = lax.all_gather(partial, 'c')  2.18 us
  transfers between devices with their start and end apart: 2, of which 1 were waited for; matrix products, arithmetic and copies ran while one was open for 0% of the time, Pallas kernels for 1%

profile of v7, /device:TPU:8, one launch (start us, length us, event | category | flops | bytes accessed | tf_op | source)
XLA Modules:
  0.0 101.2 jit_solution(13181654179988712611)
XLA Ops:
  0.6 0.0 copy-start
  0.6 2.4 %pack.1 = (bf16[8,112,512]{2,1,0:T(8,128)(2,1)}, bf16[32,512]{1,0:T(8,128)(2,1)S(1)}) custom-call(s32[1,32]{1,0:T(1,128)} %bitcast.5, bf16[1,2,32,4096]{3,2,1,0:T(8,128)(2,1)} %g_hbm.1, bf16[1,2,32,256]{3,2,1,0:T(8,128)(2,1)} %l_hbm.1), custom_call_target="tpu_custom_call" | custom-call | bytes 1048576 | tf_op jit(solution)/shard_map/pack/pallas_call | solution.py:119
  3.0 16.5 %all-to-all-start = ((bf16[8,112,512]{2,1,0:T(8,128)(2,1)}), bf16[8,112,512]{2,1,0:T(8,128)(2,1)S(1)}, u32[]{:S(2)}, u32[]{:S(2)}) async-start(bf16[8,112,512]{2,1,0:T(8,128)(2,1)} %get-tuple-element.8), calls=%async_computation | async-start | bytes 1835008 | tf_op jit(solution)/shard_map/all_to_all | solution.py:221
  19.6 36.3 %all-gather = bf16[512,512]{1,0:T(8,128)(2,1)S(1)} all-gather(bf16[32,512]{1,0:T(8,128)(2,1)S(1)} %get-tuple-element.9), channel_id=2, replica_groups=mesh['x'=4,'c'=2,'z'=16,'y'=8] {'z'}, dimensions={0}, use_global_device_ids=true | all-gather | bytes 557056 | tf_op jit(solution)/shard_map/all_gather | solution.py:222
  55.9 0.0 all-to-all-done.b_ref
  55.9 0.0 copy-done
  55.9 1.4 %shard_map.77 = bf16[256,512]{1,0:T(8,128)(2,1)S(1)} custom-call(f32[1,2]{1,0:T(1,128)} %w_ref.1, bf16[8,112,512]{2,1,0:T(8,128)(2,1)S(1)} %all-to-all-done.b_ref, bf16[16,32,512]{2,1,0:T(8,128)(2,1)S(1)} %bitcast.4, bf16[1,2,2,256]{3,2,1,0:T(2,128)(2,1)S(1)} %copy-done), custom_call_target="tpu_custom_call" | custom-call | flops 536870912 | bytes 1048576 | tf_op jit(solution)/shard_map/pallas_call | solution.py:35
  57.3 2.2 %all-gather.1 = bf16[512,512]{1,0:T(8,128)(2,1)S(1)} all-gather(bf16[256,512]{1,0:T(8,128)(2,1)S(1)} %shard_map.77), channel_id=3, replica_groups=mesh['x'=4,'c'=2,'z'=16,'y'=8] {'c'}, dimensions={0}, use_global_device_ids=true | all-gather | bytes 786432 | tf_op jit(solution)/shard_map/all_gather | solution.py:226
  59.5 0.7 shard_map.78
  60.2 4.0 %all-to-all-start.1 = ((bf16[16,16,256]{2,1,0:T(8,128)(2,1)}), bf16[16,16,256]{2,1,0:T(8,128)(2,1)S(1)}, u32[]{:S(2)}, u32[]{:S(2)}) async-start(bf16[16,16,256]{2,1,0:T(8,128)(2,1)} %get-tuple-element.10), calls=%async_computation.1 | async-start | bytes 262144 | tf_op jit(solution)/shard_map/all_to_all | solution.py:228
  64.2 1.4 %shard_map.79 = (bf16[32,8,256]{2,1,0:T(8,128)(2,1)S(1)}, bf16[256,3072]{1,0:T(8,128)(2,1)S(1)}) custom-call(bf16[8,16,128]{2,1,0:T(8,128)(2,1)S(1)} %slice.4.s_ref, bf16[256,256]{1,0:T(8,128)(2,1)S(1)} %get-tuple-element.11.d_ref, bf16[256,4096]{1,0:T(8,128)(2,1)} %refs_1_.1), custom_call_target="tpu_custom_call" | custom-call | flops 8388608 | bytes 2097152 | tf_op jit(solution)/shard_map/pallas_call | solution.py:35
  65.7 13.3 %all-to-all-done.1.q_ref = bf16[16,16,256]{2,1,0:T(8,128)(2,1)S(1)} async-done(((bf16[16,16,256]{2,1,0:T(8,128)(2,1)}), bf16[16,16,256]{2,1,0:T(8,128)(2,1)S(1)}, u32[]{:S(2)}, u32[]{:S(2)}) %all-to-all-start.1) | async-done | bytes 131104 | tf_op jit(solution)/shard_map/all_to_all | solution.py:228
  79.0 20.1 %all_to_all.15.p_ref = bf16[32,8,384]{2,1,0:T(8,128)(2,1)S(1)} all-to-all(bf16[32,8,384]{2,1,0:T(8,128)(2,1)S(1)} %shard_map.80), channel_id=1, replica_groups=mesh['x'=4,'c'=2,'z'=16,'y'=8] {'x','y'}, dimensions={0} | all-to-all | bytes 393216 | tf_op jit(solution)/shard_map/all_to_all | solution.py:238
  99.1 2.1 %shard_map.81 = (f32[2,256]{1,0:T(2,128)}, bf16[8,4096]{1,0:T(8,128)(2,1)}) custom-call(bf16[32,8,384]{2,1,0:T(8,128)(2,1)S(1)} %all_to_all.15.p_ref, bf16[256,3072]{1,0:T(8,128)(2,1)S(1)} %get-tuple-element.13.refs_0_, bf16[256,4096]{1,0:T(8,128)(2,1)} %refs_1_.1), custom_call_target="tpu_custom_call" | custom-call | flops 16777216 | bytes 262144 | tf_op jit(solution)/shard_map/pallas_call | solution.py:35
  (2 shorter events, 0.0 us)
Async XLA Ops:
  0.6 55.2 %copy-start = (bf16[1,2,2,256]{3,2,1,0:T(2,128)(2,1)S(1)}, bf16[1,2,2,256]{3,2,1,0:T(2,128)(2,1)}, u32[]{:S(2)}) copy-start(bf16[1,2,2,256]{3,2,1,0:T(2,128)(2,1)} %d_ref.1) | copy-start | bytes 6148
  3.0 52.8 %all-to-all-start = ((bf16[8,112,512]{2,1,0:T(8,128)(2,1)}), bf16[8,112,512]{2,1,0:T(8,128)(2,1)S(1)}, u32[]{:S(2)}, u32[]{:S(2)}) async-start(bf16[8,112,512]{2,1,0:T(8,128)(2,1)} %get-tuple-element.8), calls=%async_computation | async-start | bytes 1835008 | tf_op jit(solution)/shard_map/all_to_all | solution.py:221
  60.2 18.8 %all-to-all-start.1 = ((bf16[16,16,256]{2,1,0:T(8,128)(2,1)}), bf16[16,16,256]{2,1,0:T(8,128)(2,1)S(1)}, u32[]{:S(2)}, u32[]{:S(2)}) async-start(bf16[16,16,256]{2,1,0:T(8,128)(2,1)} %get-tuple-element.10), calls=%async_computation.1 | async-start | bytes 262144 | tf_op jit(solution)/shard_map/all_to_all | solution.py:228

commit v8 on v7

--- a/solution.py
+++ b/solution.py
@@ -74,7 +74,7 @@
     rows_in.wait()
     for side in range(2):
         rows = l_ref[0, side]
-        own_ref[:, W * side : W * side + W] = rows
+        own_ref[0, :, W * side : W * side + W] = rows
         for y in range(NY):
             out_ref[y, 2 * RD : 3 * RD, W * side : W * side + W] = rows
     owners_in.wait()
@@ -118,7 +118,7 @@
     anywhere = pl.BlockSpec(memory_space=pl.ANY)
     return pl.pallas_call(
         pack_kernel,
-        out_shape=(jax.ShapeDtypeStruct(packed, BF16), pltpu.VMEM((RD, 2 * W), BF16)),
+        out_shape=(jax.ShapeDtypeStruct(packed, BF16), pltpu.VMEM((1, RD, 2 * W), BF16)),
         in_specs=[anywhere] * 3,
         out_specs=(anywhere, VM),
         scratch_shapes=[
@@ -177,20 +177,21 @@
         place = (index == slot).astype(F32).astype(BF16)
         placed = jnp.dot(place, rows[RD * y : RD * y + RD], preferred_element_type=F32).astype(BF16)
         for x in range(NX):
-            out_ref[NY * x + y] = placed[CAP * x : CAP * x + CAP]
+            for part in range(2):
+                start = CAP * x + 4 * part
+                out_ref[NY * x + y, :, W * part : W * part + W] = placed[start : start + 4]
     for piece in pieces:
         piece.wait()
 
 
 def join_kernel(q_ref, p_ref, out_ref):
     quad = jnp.sum(q_ref[...].astype(F32), axis=0)
-    zero = jnp.zeros((CAP - 4, 128), F32)
-    out_ref[:, :, 0:W] = p_ref[...]
+    out_ref[:, :, 0 : 2 * W] = p_ref[...]
     for y in range(NY):
         rows = quad[2 * y : 2 * y + 2]
-        tail = jnp.concatenate([rows[:, :128], rows[:, 128:], zero], axis=0).astype(BF16)
+        tail = jnp.concatenate([rows[:, :128], rows[:, 128:]], axis=0).astype(BF16)
         for x in range(NX):
-            out_ref[NY * x + y, :, W:] = tail
+            out_ref[NY * x + y, :, 2 * W :] = tail
 
 
 def total_kernel(p_ref, *refs):
@@ -204,9 +205,9 @@
     for piece in pieces:
         piece.start()
     total = jnp.sum(p_ref[...].astype(F32), axis=0)
-    diag_ref[:, 0:128] = total[0:2, W:]
-    diag_ref[:, 128:] = total[2:4, W:]
-    half = total[:, :W].astype(BF16)
+    diag_ref[:, 0:128] = total[0:2, 2 * W :]
+    diag_ref[:, 128:] = total[2:4, 2 * W :]
+    half = jnp.concatenate([total[:, :W], total[:, W : 2 * W]], axis=0).astype(BF16)
     for i, slab in enumerate(slabs):
         span = pl.ds(HELD * i, HELD)
         energy_ref[:, span] = jnp.dot(half, slab[...], preferred_element_type=F32).astype(BF16)
@@ -219,7 +220,7 @@
 def per_device(trailing, panel, diag_inverse, pole_weights, owner_map, ham_slab):
     packed, own = pack(owner_map, trailing, panel)
     block = lax.all_to_all(packed, "y", 0, 0)
-    columns = lax.all_gather(own, "z")
+    columns = lax.all_gather(own, "z", axis=0, tiled=True)
     (partial,) = kernel_call(
         cross_kernel, [((ZR, 2 * W), BF16)], [SM, VM, VM, VM], flops=1 << 29, moved=1 << 20
     )(pole_weights, block, columns, diag_inverse)
@@ -228,13 +229,13 @@
     quad = lax.all_to_all(quad, "z", 0, 0)
     placed, *slabs = kernel_call(
         place_kernel,
-        [((NX * NY, CAP, W), BF16)] + [((W, HELD), BF16)] * HOLD,
+        [((NX * NY, 4, 2 * W), BF16)] + [((W, HELD), BF16)] * HOLD,
         [VM, VM, pl.BlockSpec(memory_space=pl.ANY)],
         flops=1 << 23,
         moved=1 << 21,
         scratch=[pltpu.SemaphoreType.DMA((HOLD,))],
     )(block[:, 3 * RD :, :128], density, ham_slab)
-    (joined,) = kernel_call(join_kernel, [((NX * NY, CAP, W + 128), BF16)], [VM, VM], moved=1 << 18)(quad, placed)
+    (joined,) = kernel_call(join_kernel, [((NX * NY, 4, 2 * W + 128), BF16)], [VM, VM], moved=1 << 18)(quad, placed)
     joined = lax.all_to_all(joined, ("x", "y"), 0, 0)
     streamed = NZ * NY * RD - HOLD * HELD
     density_diag, patch_energy = kernel_call(

time: 102 us -> 101 us (level)
  no operation moved by 1% of the time
where the time goes in v8:
time: 101 us
  blocking collectives  58.1 us (58%)
  starting transfers between devices  20.6 us (20%)
  waiting for transfers between devices  13.3 us (13%)
  Pallas kernels  8.1 us (8%)
    all_gather x1, blocking collectives, per_device(): columns = lax.all_gather(own, 'z', axis=0, tiled=True)  36.3 us
    all_to_all x1, blocking collectives, per_device(): joined = lax.all_to_all(joined, ('x', 'y'), 0, 0)  19.7 us
    all_to_all x1, starting transfers between devices, per_device(): block = lax.all_to_all(packed, 'y', 0, 0)  16.5 us
    all_to_all x1, waiting for transfers between devices, per_device(): quad = lax.all_to_all(quad, 'z', 0, 0)  13.3 us
    pallas_call x5, Pallas kernels, run(): call(*(pltpu.with_memory_space_constraint(arg, pltpu.VMEM) if spec is VM...  5.7 us
    all_to_all x1, starting transfers between devices, per_device(): quad = lax.all_to_all(quad, 'z', 0, 0)  4.04 us
    pallas_call x1, Pallas kernels, pack(): pl.pallas_call(pack_kernel, out_shape=(jax.ShapeDtypeStruct(packed, BF16)...  2.4 us
    all_gather x1, blocking collectives, per_device(): both = lax.all_gather(partial, 'c')  2.18 us
  transfers between devices with their start and end apart: 2, of which 1 were waited for; matrix products, arithmetic and copies ran while one was open for 0% of the time, Pallas kernels for 1%

profile of v8, /device:TPU:8, one launch (start us, length us, event | category | flops | bytes accessed | tf_op | source)
XLA Modules:
  0.0 100.8 jit_solution(13868329952289809821)
XLA Ops:
  0.6 0.0 copy-start
  0.6 2.4 %pack.1 = (bf16[8,112,512]{2,1,0:T(8,128)(2,1)}, bf16[1,32,512]{2,1,0:T(8,128)(2,1)S(1)}) custom-call(s32[1,32]{1,0:T(1,128)} %bitcast.3, bf16[1,2,32,4096]{3,2,1,0:T(8,128)(2,1)} %g_hbm.1, bf16[1,2,32,256]{3,2,1,0:T(8,128)(2,1)} %l_hbm.1), custom_call_target="tpu_custom_call" | custom-call | bytes 1048576 | tf_op jit(solution)/shard_map/pack/pallas_call | solution.py:119
  3.0 16.5 %all-to-all-start = ((bf16[8,112,512]{2,1,0:T(8,128)(2,1)}), bf16[8,112,512]{2,1,0:T(8,128)(2,1)S(1)}, u32[]{:S(2)}, u32[]{:S(2)}) async-start(bf16[8,112,512]{2,1,0:T(8,128)(2,1)} %get-tuple-element.8), calls=%async_computation | async-start | bytes 1835008 | tf_op jit(solution)/shard_map/all_to_all | solution.py:222
  19.6 36.3 %all_gather.9.l_ref = bf16[16,32,512]{2,1,0:T(8,128)(2,1)S(1)} all-gather(bf16[1,32,512]{2,1,0:T(8,128)(2,1)S(1)} %get-tuple-element.9), channel_id=1, replica_groups=mesh['x'=4,'c'=2,'z'=16,'y'=8] {'z'}, dimensions={0}, use_global_device_ids=true | all-gather | bytes 557056 | tf_op jit(solution)/shard_map/all_gather | solution.py:223
  55.9 0.0 all-to-all-done.b_ref
  55.9 0.0 copy-done
  55.9 1.4 %shard_map.77 = bf16[256,512]{1,0:T(8,128)(2,1)S(1)} custom-call(f32[1,2]{1,0:T(1,128)} %w_ref.1, bf16[8,112,512]{2,1,0:T(8,128)(2,1)S(1)} %all-to-all-done.b_ref, bf16[16,32,512]{2,1,0:T(8,128)(2,1)S(1)} %all_gather.9.l_ref, bf16[1,2,2,256]{3,2,1,0:T(2,128)(2,1)S(1)} %copy-done), custom_call_target="tpu_custom_call" | custom-call | flops 536870912 | bytes 1048576 | tf_op jit(solution)/shard_map/pallas_call | solution.py:35
  57.3 2.2 %all-gather = bf16[512,512]{1,0:T(8,128)(2,1)S(1)} all-gather(bf16[256,512]{1,0:T(8,128)(2,1)S(1)} %shard_map.77), channel_id=2, replica_groups=mesh['x'=4,'c'=2,'z'=16,'y'=8] {'c'}, dimensions={0}, use_global_device_ids=true | all-gather | bytes 786432 | tf_op jit(solution)/shard_map/all_gather | solution.py:227
  59.5 0.7 shard_map.78
  60.2 4.0 %all-to-all-start.1 = ((bf16[16,16,256]{2,1,0:T(8,128)(2,1)}), bf16[16,16,256]{2,1,0:T(8,128)(2,1)S(1)}, u32[]{:S(2)}, u32[]{:S(2)}) async-start(bf16[16,16,256]{2,1,0:T(8,128)(2,1)} %get-tuple-element.10), calls=%async_computation.1 | async-start | bytes 262144 | tf_op jit(solution)/shard_map/all_to_all | solution.py:229
  64.2 1.4 %shard_map.79 = (bf16[32,4,512]{2,1,0:T(4,128)(2,1)S(1)}, bf16[256,3072]{1,0:T(8,128)(2,1)S(1)}) custom-call(bf16[8,16,128]{2,1,0:T(8,128)(2,1)S(1)} %slice.4.s_ref, bf16[256,256]{1,0:T(8,128)(2,1)S(1)} %get-tuple-element.11.d_ref, bf16[256,4096]{1,0:T(8,128)(2,1)} %refs_1_.1), custom_call_target="tpu_custom_call" | custom-call | flops 8388608 | bytes 2097152 | tf_op jit(solution)/shard_map/pallas_call | solution.py:35
  65.7 13.3 %all-to-all-done.1.q_ref = bf16[16,16,256]{2,1,0:T(8,128)(2,1)S(1)} async-done(((bf16[16,16,256]{2,1,0:T(8,128)(2,1)}), bf16[16,16,256]{2,1,0:T(8,128)(2,1)S(1)}, u32[]{:S(2)}, u32[]{:S(2)}) %all-to-all-start.1) | async-done | bytes 131104 | tf_op jit(solution)/shard_map/all_to_all | solution.py:229
  79.0 19.7 %all_to_all.15.p_ref = bf16[32,4,640]{2,1,0:T(4,128)(2,1)S(1)} all-to-all(bf16[32,4,640]{2,1,0:T(4,128)(2,1)S(1)} %shard_map.80), channel_id=1, replica_groups=mesh['x'=4,'c'=2,'z'=16,'y'=8] {'x','y'}, dimensions={0} | all-to-all | bytes 327680 | tf_op jit(solution)/shard_map/all_to_all | solution.py:239
  98.7 2.1 %shard_map.81 = (f32[2,256]{1,0:T(2,128)}, bf16[8,4096]{1,0:T(8,128)(2,1)}) custom-call(bf16[32,4,640]{2,1,0:T(4,128)(2,1)S(1)} %all_to_all.15.p_ref, bf16[256,3072]{1,0:T(8,128)(2,1)S(1)} %get-tuple-element.13.refs_0_, bf16[256,4096]{1,0:T(8,128)(2,1)} %refs_1_.1), custom_call_target="tpu_custom_call" | custom-call | flops 16777216 | bytes 262144 | tf_op jit(solution)/shard_map/pallas_call | solution.py:35
  (2 shorter events, 0.0 us)
Async XLA Ops:
  0.6 55.2 %copy-start = (bf16[1,2,2,256]{3,2,1,0:T(2,128)(2,1)S(1)}, bf16[1,2,2,256]{3,2,1,0:T(2,128)(2,1)}, u32[]{:S(2)}) copy-start(bf16[1,2,2,256]{3,2,1,0:T(2,128)(2,1)} %d_ref.1) | copy-start | bytes 6148
  3.0 52.8 %all-to-all-start = ((bf16[8,112,512]{2,1,0:T(8,128)(2,1)}), bf16[8,112,512]{2,1,0:T(8,128)(2,1)S(1)}, u32[]{:S(2)}, u32[]{:S(2)}) async-start(bf16[8,112,512]{2,1,0:T(8,128)(2,1)} %get-tuple-element.8), calls=%async_computation | async-start | bytes 1835008 | tf_op jit(solution)/shard_map/all_to_all | solution.py:222
  60.2 18.8 %all-to-all-start.1 = ((bf16[16,16,256]{2,1,0:T(8,128)(2,1)}), bf16[16,16,256]{2,1,0:T(8,128)(2,1)S(1)}, u32[]{:S(2)}, u32[]{:S(2)}) async-start(bf16[16,16,256]{2,1,0:T(8,128)(2,1)} %get-tuple-element.10), calls=%async_computation.1 | async-start | bytes 262144 | tf_op jit(solution)/shard_map/all_to_all | solution.py:229

commit v9 on v8

--- a/solution.py
+++ b/solution.py
@@ -14,7 +14,6 @@
 TAIL = 16
 HOLD = 1
 HELD = 3072
-PIECE = 1024
 F32 = jnp.float32
 BF16 = jnp.bfloat16
 VM = pl.BlockSpec(memory_space=pltpu.VMEM)
@@ -194,27 +193,46 @@
             out_ref[NY * x + y, :, 2 * W :] = tail
 
 
-def total_kernel(p_ref, *refs):
-    slabs, (h_hbm, diag_ref, energy_ref, h_ref, sem) = refs[:HOLD], refs[HOLD:]
-    held = HOLD * HELD
-    spans = [pl.ds(start, PIECE) for start in range(0, NZ * NY * RD - held, PIECE)]
+def total_kernel(p_ref, h_ref, h_hbm, diag_ref, energy_hbm, rest_ref, energy_ref, in_sem, out_sem):
+    width = NZ * NY * RD
+    rest_in = pltpu.make_async_copy(h_hbm.at[:, pl.ds(HELD, width - HELD)], rest_ref, in_sem)
+    rest_in.start()
+    total = jnp.sum(p_ref[...].astype(F32), axis=0)
+    half = jnp.concatenate([total[:, :W], total[:, W : 2 * W]], axis=0).astype(BF16)
+    spans = ((0, HELD), (HELD, width - HELD))
     pieces = [
-        pltpu.make_async_copy(h_hbm.at[:, pl.ds(held + PIECE * i, PIECE)], h_ref.at[:, span], sem.at[i])
+        pltpu.make_async_copy(energy_ref.at[:, pl.ds(*span)], energy_hbm.at[:, pl.ds(*span)], out_sem.at[i])
         for i, span in enumerate(spans)
     ]
-    for piece in pieces:
-        piece.start()
-    total = jnp.sum(p_ref[...].astype(F32), axis=0)
+    energy_ref[:, 0:HELD] = jnp.dot(half, h_ref[...], preferred_element_type=F32).astype(BF16)
+    pieces[0].start()
+    rest_in.wait()
+    energy_ref[:, HELD:] = jnp.dot(half, rest_ref[...], preferred_element_type=F32).astype(BF16)
+    pieces[1].start()
     diag_ref[:, 0:128] = total[0:2, 2 * W :]
     diag_ref[:, 128:] = total[2:4, 2 * W :]
-    half = jnp.concatenate([total[:, :W], total[:, W : 2 * W]], axis=0).astype(BF16)
-    for i, slab in enumerate(slabs):
-        span = pl.ds(HELD * i, HELD)
-        energy_ref[:, span] = jnp.dot(half, slab[...], preferred_element_type=F32).astype(BF16)
-    for i, (piece, span) in enumerate(zip(pieces, spans, strict=True)):
+    for piece in pieces:
         piece.wait()
-        to = pl.ds(held + PIECE * i, PIECE)
-        energy_ref[:, to] = jnp.dot(half, h_ref[:, span], preferred_element_type=F32).astype(BF16)
+
+
+def energies(joined, slab, ham_slab):
+    width = NZ * NY * RD
+    anywhere = pl.BlockSpec(memory_space=pl.ANY)
+    joined, slab = (pltpu.with_memory_space_constraint(value, pltpu.VMEM) for value in (joined, slab))
+    return pl.pallas_call(
+        total_kernel,
+        out_shape=(jax.ShapeDtypeStruct((2, W), F32), jax.ShapeDtypeStruct((CAP, width), BF16)),
+        in_specs=[VM, VM, anywhere],
+        out_specs=(VM, anywhere),
+        scratch_shapes=[
+            pltpu.VMEM((W, width - HELD), BF16),
+            pltpu.VMEM((CAP, width), BF16),
+            pltpu.SemaphoreType.DMA,
+            pltpu.SemaphoreType.DMA((2,)),
+        ],
+        name="total",
+        cost_estimate=pl.CostEstimate(flops=1 << 24, bytes_accessed=1 << 18, transcendentals=0),
+    )(joined, slab, ham_slab)
 
 
 def per_device(trailing, panel, diag_inverse, pole_weights, owner_map, ham_slab):
@@ -237,16 +255,7 @@
     )(block[:, 3 * RD :, :128], density, ham_slab)
     (joined,) = kernel_call(join_kernel, [((NX * NY, 4, 2 * W + 128), BF16)], [VM, VM], moved=1 << 18)(quad, placed)
     joined = lax.all_to_all(joined, ("x", "y"), 0, 0)
-    streamed = NZ * NY * RD - HOLD * HELD
-    density_diag, patch_energy = kernel_call(
-        total_kernel,
-        [((2, W), F32), ((CAP, NZ * NY * RD), BF16)],
-        [VM] * (1 + HOLD) + [pl.BlockSpec(memory_space=pl.ANY)],
-        flops=1 << 24,
-        moved=1 << 18,
-        kept=(False, False),
-        scratch=[pltpu.VMEM((W, streamed), BF16), pltpu.SemaphoreType.DMA((streamed // PIECE,))],
-    )(joined, *slabs, ham_slab)
+    density_diag, patch_energy = energies(joined, slabs[0], ham_slab)
     return (density_diag, patch_energy)
 
 

time: 101 us -> 102 us (level)
    pallas_call x0 -> x1, Pallas kernels: none -> 2.71 us  [energies(): pl.pallas_call(total_kernel, out_shape=(jax.ShapeDtypeStruct((2, W), F32)...]
    pallas_call x5 -> x4, Pallas kernels: 5.7 us -> 3.58 us  [run(): call(*(pltpu.with_memory_space_constraint(arg, pltpu.VMEM) if spec is VM...]
where the time goes in v9:
time: 102 us; the launch traced here: 101 us
  blocking collectives  58.1 us (57%)
  starting transfers between devices  20.6 us (20%)
  waiting for transfers between devices  13.3 us (13%)
  Pallas kernels  8.69 us (9%)
    all_gather x1, blocking collectives, per_device(): columns = lax.all_gather(own, 'z', axis=0, tiled=True)  36.3 us
    all_to_all x1, blocking collectives, per_device(): joined = lax.all_to_all(joined, ('x', 'y'), 0, 0)  19.7 us
    all_to_all x1, starting transfers between devices, per_device(): block = lax.all_to_all(packed, 'y', 0, 0)  16.5 us
    all_to_all x1, waiting for transfers between devices, per_device(): quad = lax.all_to_all(quad, 'z', 0, 0)  13.3 us
    all_to_all x1, starting transfers between devices, per_device(): quad = lax.all_to_all(quad, 'z', 0, 0)  4.04 us
    pallas_call x4, Pallas kernels, run(): call(*(pltpu.with_memory_space_constraint(arg, pltpu.VMEM) if spec is VM...  3.58 us
    pallas_call x1, Pallas kernels, energies(): pl.pallas_call(total_kernel, out_shape=(jax.ShapeDtypeStruct((2, W), F32)...  2.71 us
    pallas_call x1, Pallas kernels, pack(): pl.pallas_call(pack_kernel, out_shape=(jax.ShapeDtypeStruct(packed, BF16)...  2.4 us
  transfers between devices with their start and end apart: 2, of which 1 were waited for; matrix products, arithmetic and copies ran while one was open for 0% of the time, Pallas kernels for 1%

profile of v9, /device:TPU:8, one launch (start us, length us, event | category | flops | bytes accessed | tf_op | source)
XLA Modules:
  0.0 101.4 jit_solution(15103930152401928730)
XLA Ops:
  0.6 0.0 copy-start
  0.6 2.4 %pack.1 = (bf16[8,112,512]{2,1,0:T(8,128)(2,1)}, bf16[1,32,512]{2,1,0:T(8,128)(2,1)S(1)}) custom-call(s32[1,32]{1,0:T(1,128)} %bitcast.3, bf16[1,2,32,4096]{3,2,1,0:T(8,128)(2,1)} %g_hbm.1, bf16[1,2,32,256]{3,2,1,0:T(8,128)(2,1)} %l_hbm.1), custom_call_target="tpu_custom_call" | custom-call | bytes 1048576 | tf_op jit(solution)/shard_map/pack/pallas_call | solution.py:118
  3.0 16.5 %all-to-all-start = ((bf16[8,112,512]{2,1,0:T(8,128)(2,1)}), bf16[8,112,512]{2,1,0:T(8,128)(2,1)S(1)}, u32[]{:S(2)}, u32[]{:S(2)}) async-start(bf16[8,112,512]{2,1,0:T(8,128)(2,1)} %get-tuple-element.8), calls=%async_computation | async-start | bytes 1835008 | tf_op jit(solution)/shard_map/all_to_all | solution.py:240
  19.6 36.3 %all_gather.9.l_ref = bf16[16,32,512]{2,1,0:T(8,128)(2,1)S(1)} all-gather(bf16[1,32,512]{2,1,0:T(8,128)(2,1)S(1)} %get-tuple-element.9), channel_id=1, replica_groups=mesh['x'=4,'c'=2,'z'=16,'y'=8] {'z'}, dimensions={0}, use_global_device_ids=true | all-gather | bytes 557056 | tf_op jit(solution)/shard_map/all_gather | solution.py:241
  55.9 0.0 all-to-all-done.b_ref
  55.9 0.0 copy-done
  55.9 1.4 %shard_map.77 = bf16[256,512]{1,0:T(8,128)(2,1)S(1)} custom-call(f32[1,2]{1,0:T(1,128)} %w_ref.1, bf16[8,112,512]{2,1,0:T(8,128)(2,1)S(1)} %all-to-all-done.b_ref, bf16[16,32,512]{2,1,0:T(8,128)(2,1)S(1)} %all_gather.9.l_ref, bf16[1,2,2,256]{3,2,1,0:T(2,128)(2,1)S(1)} %copy-done), custom_call_target="tpu_custom_call" | custom-call | flops 536870912 | bytes 1048576 | tf_op jit(solution)/shard_map/pallas_call | solution.py:34
  57.3 2.2 %all-gather = bf16[512,512]{1,0:T(8,128)(2,1)S(1)} all-gather(bf16[256,512]{1,0:T(8,128)(2,1)S(1)} %shard_map.77), channel_id=2, replica_groups=mesh['x'=4,'c'=2,'z'=16,'y'=8] {'c'}, dimensions={0}, use_global_device_ids=true | all-gather | bytes 786432 | tf_op jit(solution)/shard_map/all_gather | solution.py:245
  59.5 0.7 shard_map.78
  60.2 4.0 %all-to-all-start.1 = ((bf16[16,16,256]{2,1,0:T(8,128)(2,1)}), bf16[16,16,256]{2,1,0:T(8,128)(2,1)S(1)}, u32[]{:S(2)}, u32[]{:S(2)}) async-start(bf16[16,16,256]{2,1,0:T(8,128)(2,1)} %get-tuple-element.10), calls=%async_computation.1 | async-start | bytes 262144 | tf_op jit(solution)/shard_map/all_to_all | solution.py:247
  64.2 1.4 %shard_map.79 = (bf16[32,4,512]{2,1,0:T(4,128)(2,1)S(1)}, bf16[256,3072]{1,0:T(8,128)(2,1)S(1)}) custom-call(bf16[8,16,128]{2,1,0:T(8,128)(2,1)S(1)} %slice.4.s_ref, bf16[256,256]{1,0:T(8,128)(2,1)S(1)} %get-tuple-element.11.d_ref, bf16[256,4096]{1,0:T(8,128)(2,1)} %h_hbm.3), custom_call_target="tpu_custom_call" | custom-call | flops 8388608 | bytes 2097152 | tf_op jit(solution)/shard_map/pallas_call | solution.py:34
  65.7 13.3 %all-to-all-done.1.q_ref = bf16[16,16,256]{2,1,0:T(8,128)(2,1)S(1)} async-done(((bf16[16,16,256]{2,1,0:T(8,128)(2,1)}), bf16[16,16,256]{2,1,0:T(8,128)(2,1)S(1)}, u32[]{:S(2)}, u32[]{:S(2)}) %all-to-all-start.1) | async-done | bytes 131104 | tf_op jit(solution)/shard_map/all_to_all | solution.py:247
  79.0 19.7 %all_to_all.15.p_ref = bf16[32,4,640]{2,1,0:T(4,128)(2,1)S(1)} all-to-all(bf16[32,4,640]{2,1,0:T(4,128)(2,1)S(1)} %shard_map.80), channel_id=1, replica_groups=mesh['x'=4,'c'=2,'z'=16,'y'=8] {'x','y'}, dimensions={0} | all-to-all | bytes 327680 | tf_op jit(solution)/shard_map/all_to_all | solution.py:257
  98.7 2.7 %total.1 = (f32[2,256]{1,0:T(2,128)}, bf16[8,4096]{1,0:T(8,128)(2,1)}) custom-call(bf16[32,4,640]{2,1,0:T(4,128)(2,1)S(1)} %all_to_all.15.p_ref, bf16[256,3072]{1,0:T(8,128)(2,1)S(1)} %get-tuple-element.13.h_ref, bf16[256,4096]{1,0:T(8,128)(2,1)} %h_hbm.3), custom_call_target="tpu_custom_call" | custom-call | flops 16777216 | bytes 262144 | tf_op jit(solution)/shard_map/total/pallas_call | solution.py:222
  (2 shorter events, 0.0 us)
Async XLA Ops:
  0.6 55.2 %copy-start = (bf16[1,2,2,256]{3,2,1,0:T(2,128)(2,1)S(1)}, bf16[1,2,2,256]{3,2,1,0:T(2,128)(2,1)}, u32[]{:S(2)}) copy-start(bf16[1,2,2,256]{3,2,1,0:T(2,128)(2,1)} %d_ref.1) | copy-start | bytes 6148
  3.0 52.8 %all-to-all-start = ((bf16[8,112,512]{2,1,0:T(8,128)(2,1)}), bf16[8,112,512]{2,1,0:T(8,128)(2,1)S(1)}, u32[]{:S(2)}, u32[]{:S(2)}) async-start(bf16[8,112,512]{2,1,0:T(8,128)(2,1)} %get-tuple-element.8), calls=%async_computation | async-start | bytes 1835008 | tf_op jit(solution)/shard_map/all_to_all | solution.py:240
  60.2 18.8 %all-to-all-start.1 = ((bf16[16,16,256]{2,1,0:T(8,128)(2,1)}), bf16[16,16,256]{2,1,0:T(8,128)(2,1)S(1)}, u32[]{:S(2)}, u32[]{:S(2)}) async-start(bf16[16,16,256]{2,1,0:T(8,128)(2,1)} %get-tuple-element.10), calls=%async_computation.1 | async-start | bytes 262144 | tf_op jit(solution)/shard_map/all_to_all | solution.py:247
